TPU v7x, 32 devices: a whole 2x2x4 slice. The times are simulated.
32 devices in a mesh: dp: 8 (over y, x, core), mp: 4 (over z).
Axes of the slice: x: 2, y: 2, z: 4, core: 2. Of those that a mesh axis runs over, the one named last changes fastest.
Arguments:
- hidden: bfloat16 [192, 256, 4096], P(('dp', 'mp')), may hold values from -6 to 6
- lengths: int32 [192], P(('dp', 'mp')), may hold values from 32 to 256, as said below
- list_ids: int32 [192], P('dp'), may hold values from 0 to 65535, as said below
- gain: bfloat16 [4096], replicated, may hold values from 0.099609375 to 1.8984375
- head: bfloat16 [4096, 1024], P('dp', 'mp'), may hold values from -0.09375 to 0.09375
- list_slot: int32 [65536], replicated, may hold values from 0 to 65535, as said below
- centroids: bfloat16 [65536, 1024], P('dp'), may hold values from -0.59765625 to 0.59765625
- rotation: bfloat16 [1024, 1024], P('mp'), may hold values from -0.1875 to 0.1875
Outputs:
- codes: bfloat16 [192, 1024], P('dp', 'mp')
- scales: bfloat16 [192, 16], P('dp', 'mp')
Inputs may be any that keep to these rules, and one draw needn't show every extreme that they name: `list_ids`: in each aligned block of 24 passages, at most 6 have lists in one range of 8192 lists (list id // 8192); one range holds exactly 6 of them in every block. Each list's row in the centroid table; list_slot[l] // 8192 equals l // 8192, and each row of a range once. `lengths`: some passage has exactly 256 valid tokens.
All inputs are finite; a program needn't handle non-finite values. Where the computation divides by a largest or mean magnitude, that divisor is 1e-20 or more.
Results may differ from a plain program's by a relative error of at most 0.013.
Values may be sent and summed in bfloat16 or wider, within the bound.
No kernel may reach another device: no remote copies, remote signals or barrier semaphores. Data moves between devices by JAX's collectives and lax.ppermute only.
A program may use at most 64 MiB of HBM per device.

v0:
```python
import functools

import jax
import jax.numpy as jnp
from jax import lax
from jax.experimental import pallas as pl
from jax.experimental.pallas import tpu as pltpu
from jax.sharding import Mesh
from jax.sharding import PartitionSpec as P

BLOCK = 64
LANES = 128
SUB = 8
DIGIT = 256
CORES = 2
STEP = 64

F32 = jnp.float32
BF16 = jnp.bfloat16


def near(x):
    return pltpu.with_memory_space_constraint(x, pltpu.VMEM)


def pool_kernel(
    lens, ids, hidden, slots, gain, out, buf, weight, acc, slot_rows, items, counts, sems, slot_sem,
    *, owners, peers, lists_own, capacity, lead,
):
    passes, length, width = hidden.shape
    group = ids.shape[0]
    steps = length // STEP
    tiles = width // LANES
    rows = out.shape[1] * owners // tiles

    def slot_copy(g):
        return pltpu.make_async_copy(
            slots.at[pl.ds(ids[g] // LANES, 1)], slot_rows.at[pl.ds(g, 1)], slot_sem
        )

    def chunk_copy(p, c):
        return pltpu.make_async_copy(
            hidden.at[p, pl.ds(c * STEP, STEP)], buf.at[p * steps + c], sems.at[p * steps + c]
        )

    count = jnp.int32(0)
    for p in range(passes):
        for c in range(steps):
            needed = c * STEP < lens[p]

            @pl.when(needed)
            def _():
                chunk_copy(p, c).start()
                items[count] = p * steps + c

            count = count + needed.astype(jnp.int32)
    for g in range(group):
        slot_copy(g).start()
    for o in range(owners):
        counts[o] = 0

    def zero(p, _):
        acc[p] = jnp.zeros((SUB, width), F32)
        return 0

    lax.fori_loop(0, passes, zero, 0)
    sub = lax.broadcasted_iota(jnp.int32, (SUB, LANES), 0)

    def arrive(k):
        item = items[k]
        pltpu.make_async_copy(
            hidden.at[0, pl.ds(0, STEP)], buf.at[item], sems.at[item]
        ).wait()

    def weigh(k):
        item = items[k]
        p = item // steps
        start = (item % steps) * STEP
        size = lens[p]
        for s in range(0, STEP, 16):
            total = None
            for t in range(tiles):
                x = buf[item, s : s + 16, t * LANES : (t + 1) * LANES].astype(F32)
                total = x * x if total is None else total + x * x
            square = jnp.sum(total, axis=1, keepdims=True)
            token = lax.broadcasted_iota(jnp.int32, (16, 1), 0) + (start + s)
            value = jnp.where(token < size, lax.rsqrt(square / width + 1e-05), 0.0)
            weight[k % 2, s : s + 16, :] = jnp.broadcast_to(value, (16, LANES))

    def add(k):
        item = items[k]
        p = item // steps
        w = weight[k % 2]
        for t in range(tiles):
            x = buf[item, :, t * LANES : (t + 1) * LANES].astype(F32) * w
            part = x[0:SUB]
            for s in range(SUB, STEP, SUB):
                part = part + x[s : s + SUB]
            acc[p, :, t * LANES : (t + 1) * LANES] += part

    arrive(0)
    weigh(0)

    def body(k, _):
        later = jnp.minimum(k + 1, count - 1)

        @pl.when(k + 1 < count)
        def _():
            arrive(k + 1)

        add(k)
        weigh(later)
        return 0

    lax.fori_loop(0, count - 1, body, 0)
    add(count - 1)

    for g in range(group):
        slot_copy(g).wait()
    owner_row = lax.broadcasted_iota(jnp.int32, (lead, LANES), 0)
    lane = lax.broadcasted_iota(jnp.int32, (lead, LANES), 1)
    info = jnp.zeros((lead, LANES), F32)
    for g in range(group):
        slot = slot_rows[g, ids[g] % LANES]
        owner = slot // lists_own
        local = slot % lists_own
        rank = counts[owner]
        counts[owner] = rank + 1
        place = (g // passes) * rows + g % passes + 1
        for kind, value in enumerate((local // DIGIT, local % DIGIT, jnp.int32(place))):
            here = (owner_row == owner) & (lane == kind * capacity + rank)
            info = jnp.where(here, value.astype(F32), info)

    per = tiles // owners
    for o in range(owners):
        for q in range(per):
            t = o * per + q
            cols = slice(t * LANES, (t + 1) * LANES)
            scale = gain[t : t + 1].astype(F32)
            tile = jnp.zeros((rows, LANES), F32)
            row = lax.broadcasted_iota(jnp.int32, (rows, LANES), 0)
            for p in range(passes):
                line = jnp.sum(acc[p, :, cols], axis=0, keepdims=True) * scale
                line = line / lens[p].astype(F32)
                tile = jnp.where(row == p, jnp.broadcast_to(line, (rows, LANES)), tile)
            if q == 0:
                line = info[o : o + 1]
                tile = jnp.where(row == passes, jnp.broadcast_to(line, (rows, LANES)), tile)
            tile = tile.astype(BF16)
            for j in range(peers):
                out[o * peers + j, q * rows : (q + 1) * rows, :] = tile


def project_kernel(
    got, head, cents, own, other, info_v, info_s, acc, rows_in, spread, packed, info_sem, sem,
    *, owners, peers, passes, capacity, rows,
):
    width = head.shape[1]
    lists_own = cents.shape[0]
    col = pl.multiple_of(lax.axis_index("mp") * width, LANES)
    per = got.shape[1] // rows
    for o in range(owners):
        line = got[o * peers, 0:rows, :].astype(F32)[passes : passes + 1]
        info_v[o : o + 1, :] = line.astype(jnp.int32)
    info_copy = pltpu.make_async_copy(info_v, info_s, info_sem)
    info_copy.start()
    total = None
    for q in range(per):
        x = got[:, q * rows : (q + 1) * rows, :].reshape(owners * peers * rows, LANES)
        y = jnp.dot(x, head[q * LANES : (q + 1) * LANES, :], preferred_element_type=F32)
        total = y if total is None else total + y
    acc[...] = total.reshape(owners, peers * rows, width)
    spread[...] = jnp.zeros(spread.shape, F32)
    info_copy.wait()

    def local_row(o, k):
        value = info_s[o, k] * DIGIT + info_s[o, capacity + k]
        return jnp.clip(value, 0, lists_own - 1)

    def row_copy(o, k, first):
        return pltpu.make_async_copy(
            cents.at[pl.ds(pl.multiple_of(first, SUB), SUB), pl.ds(col, width)],
            rows_in.at[o * capacity + k],
            sem.at[o * capacity + k],
        )

    for o in range(owners):
        for k in range(capacity):
            row_copy(o, k, (local_row(o, k) // SUB) * SUB).start()
    sub = lax.broadcasted_iota(jnp.int32, (SUB, width), 0)
    for o in range(owners):
        for k in range(capacity):
            row_copy(o, k, 0).wait()
    for o in range(owners):
        for k in range(capacity):
            place = info_s[o, 2 * capacity + k]
            place = jnp.where(place > 0, place - 1, peers * rows)
            place = jnp.clip(place, 0, peers * rows)
            tile = rows_in[o * capacity + k].astype(F32)
            line = jnp.sum(jnp.where(sub == local_row(o, k) % SUB, tile, 0.0), axis=0, keepdims=True)
            spread[o, pl.ds(place, 1), :] = line
    core = lax.axis_index("core")
    group = peers * passes
    for side in range(CORES):
        for c in range(owners // CORES):
            o = c * CORES + (core if side == 0 else 1 - core)
            x = acc[o] - spread[o, 0 : peers * rows, :]
            for j in range(peers):
                at = c * group + j * passes
                packed[side, at : at + passes, :] = x[j * rows : j * rows + passes]
    own[...] = packed[0]
    other[...] = packed[1].astype(BF16)


def rotate_kernel(own, other, rotation, out, *, peers):
    group = out.shape[1]
    width = out.shape[2]
    resid = (own[...] + other[...].astype(F32)).astype(BF16)
    for j in range(peers):
        y = jnp.dot(
            resid, rotation[:, j * width : (j + 1) * width], preferred_element_type=F32
        ).astype(BF16)
        for c in range(resid.shape[0] // group):
            out[c * peers + j] = y[c * group : (c + 1) * group]


def quantize_kernel(parts, codes, scales):
    total = parts[0].astype(F32)
    for s in range(1, parts.shape[0]):
        total = total + parts[s].astype(F32)
    group, width = total.shape
    lane = lax.broadcasted_iota(jnp.int32, (group, LANES), 1)
    table = jnp.zeros((group, LANES), F32)
    for t in range(width // LANES):
        x = total[:, t * LANES : (t + 1) * LANES]
        size = jnp.abs(x)
        spread = jnp.zeros((group, LANES), F32)
        for b in range(LANES // BLOCK):
            inside = (lane >= b * BLOCK) & (lane < (b + 1) * BLOCK)
            top = jnp.max(jnp.where(inside, size, 0.0), axis=1, keepdims=True) + 1e-06
            spread = jnp.where(inside, top, spread)
            table = jnp.where(lane == t * (LANES // BLOCK) + b, top, table)
        codes[:, t * LANES : (t + 1) * LANES] = (x / spread).astype(BF16)
    scales[...] = table.T[: scales.shape[0]].astype(BF16)


def per_device(hidden, lengths, list_ids, gain, head, list_slot, centroids, rotation):
    passes, length, width = hidden.shape
    owners = lax.axis_size("chip") * lax.axis_size("core")
    peers = lax.axis_size("mp")
    group = list_ids.shape[0]
    lists_own = centroids.shape[0]
    capacity = max(2, 2 * group // owners)
    rows = -(-(passes + 1) // SUB) * SUB
    per = width // LANES // owners
    cols = head.shape[1]
    lead = -(-owners // SUB) * SUB
    steps = length // STEP
    vmem = pl.BlockSpec(memory_space=pltpu.VMEM)
    smem = pl.BlockSpec(memory_space=pltpu.SMEM)
    hbm = pl.BlockSpec(memory_space=pl.ANY)
    blocks = pl.pallas_call(
        functools.partial(
            pool_kernel, owners=owners, peers=peers, lists_own=lists_own, capacity=capacity, lead=lead
        ),
        out_shape=pltpu.VMEM((owners * peers, per * rows, LANES), BF16),
        in_specs=[smem, smem, hbm, hbm, vmem],
        out_specs=vmem,
        scratch_shapes=[
            pltpu.VMEM((passes * steps, STEP, width), BF16),
            pltpu.VMEM((2, STEP, LANES), F32),
            pltpu.VMEM((passes, SUB, width), F32),
            pltpu.SMEM((group, LANES), jnp.int32),
            pltpu.SMEM((passes * steps,), jnp.int32),
            pltpu.SMEM((owners,), jnp.int32),
            pltpu.SemaphoreType.DMA((passes * steps,)),
            pltpu.SemaphoreType.DMA,
        ],
        compiler_params=pltpu.CompilerParams(vmem_limit_bytes=hidden.size * 2 + 6 * 2**20),
        name="pool",
    )(lengths, list_ids, hidden, list_slot.reshape(-1, LANES), gain.reshape(-1, LANES))
    got = lax.all_to_all(blocks, ("chip", "core", "mp"), 0, 0, tiled=True)
    half = owners // CORES * group
    own, other = pl.pallas_call(
        functools.partial(
            project_kernel, owners=owners, peers=peers, passes=passes, capacity=capacity, rows=rows
        ),
        out_shape=(
            pltpu.VMEM((half, cols), F32),
            pltpu.VMEM((half, cols), BF16),
        ),
        in_specs=[vmem, vmem, hbm],
        out_specs=(vmem, vmem),
        scratch_shapes=[
            pltpu.VMEM((lead, LANES), jnp.int32),
            pltpu.SMEM((lead, LANES), jnp.int32),
            pltpu.VMEM((owners, peers * rows, cols), F32),
            pltpu.VMEM((owners * capacity, SUB, cols), BF16),
            pltpu.VMEM((owners, peers * rows + SUB, cols), F32),
            pltpu.VMEM((CORES, half, cols), F32),
            pltpu.SemaphoreType.DMA,
            pltpu.SemaphoreType.DMA((owners * capacity,)),
        ],
        compiler_params=pltpu.CompilerParams(vmem_limit_bytes=8 * 2**20),
        name="project",
    )(near(got), near(head), centroids)
    other = lax.ppermute(other, "core", [(c, (c + 1) % CORES) for c in range(CORES)])
    parts = pl.pallas_call(
        functools.partial(rotate_kernel, peers=peers),
        out_shape=pltpu.VMEM((owners // CORES * peers, group, cols), BF16),
        in_specs=[vmem, vmem, vmem],
        out_specs=vmem,
        compiler_params=pltpu.CompilerParams(vmem_limit_bytes=8 * 2**20),
        name="rotate",
    )(near(own), near(other), near(rotation))
    parts = lax.all_to_all(parts, ("chip", "mp"), 0, 0, tiled=True)
    codes, scales = pl.pallas_call(
        quantize_kernel,
        out_shape=(
            jax.ShapeDtypeStruct((group, cols), BF16),
            jax.ShapeDtypeStruct((cols // BLOCK, group), BF16),
        ),
        in_specs=[vmem],
        out_specs=(vmem, vmem),
        compiler_params=pltpu.CompilerParams(vmem_limit_bytes=8 * 2**20),
        name="quantize",
    )(near(parts))
    return codes, scales.T


def solution(mesh):
    dp, mp = mesh.shape["dp"], mesh.shape["mp"]
    split = Mesh(mesh.devices.reshape(dp // CORES, CORES, mp), ("chip", "core", "mp"))
    rows = ("chip", "core")
    in_specs = (
        P(("chip", "core", "mp"), None, None),
        P(("chip", "core", "mp")),
        P(rows),
        P(),
        P(rows, "mp"),
        P(),
        P(rows, None),
        P("mp", None),
    )
    out_specs = (P(rows, "mp"), P(rows, "mp"))
    return jax.shard_map(
        per_device, mesh=split, in_specs=in_specs, out_specs=out_specs, check_vma=False
    )
```

profile of v0, /device:TPU:0, one launch (start us, length us, event | category | flops | bytes accessed | tf_op | source)
XLA Modules:
  0.0 57.0 jit_solution(14507990459997229384)
XLA Ops:
  0.6 0.0 copy-start.1
  0.6 4.6 %copy-done.1 = bf16[6,256,4096]{2,1,0:T(8,128)(2,1)S(1)} copy-done((bf16[6,256,4096]{2,1,0:T(8,128)(2,1)S(1)}, bf16[6,256,4096]{2,1,0:T(8,128)(2,1)}, u32[]{:S(2)}) %copy-start.1) | copy-done | bytes 12582936
  5.2 0.0 copy-start.4
  5.2 0.9 %copy-done.4 = s32[65536]{0:T(1024)S(1)} copy-done((s32[65536]{0:T(1024)S(1)}, s32[65536]{0:T(1024)}, u32[]{:S(2)}) %copy-start.4) | copy-done | bytes 262168
  6.2 0.0 copy-start.5
  6.2 0.7 %copy-done.5 = bf16[4096]{0:T(1024)(128)(2,1)S(1)} copy-done((bf16[4096]{0:T(1024)(128)(2,1)S(1)}, bf16[4096]{0:T(1024)(128)(2,1)}, u32[]{:S(2)}) %copy-start.5) | copy-done | bytes 8216
  6.9 0.0 copy-start.6
  6.9 0.7 %copy-done.6 = s32[6]{0:T(128)S(1)} copy-done((s32[6]{0:T(128)S(1)}, s32[6]{0:T(128)}, u32[]{:S(2)}) %copy-start.6) | copy-done | bytes 48
  7.5 0.0 copy-start.7
  7.5 0.7 %copy-done.7 = s32[24]{0:T(128)S(1)} copy-done((s32[24]{0:T(128)S(1)}, s32[24]{0:T(128)}, u32[]{:S(2)}) %copy-start.7) | copy-done | bytes 120
  8.2 0.0 copy-start.2
  8.2 5.5 %pool.1 = bf16[32,32,128]{2,1,0:T(8,128)(2,1)S(1)} custom-call(s32[6]{0:T(128)S(1)} %copy-done.6, s32[24]{0:T(128)S(1)} %copy-done.7, bf16[6,256,4096]{2,1,0:T(8,128)(2,1)S(1)} %copy-done.1, s32[512,128]{1,0:T(8,128)S(1)} %bitcast.3, bf16[32,128]{1,0:T(8,128)(2,1)S(1)} %bitcast.4), custom_call_target="tpu_custom_call" | custom-call | tf_op jit(solution)/shard_map/pool/pallas_call | solution.py:262
  13.7 18.9 %all_to_all.10.got = bf16[32,32,128]{2,1,0:T(8,128)(2,1)S(1)} all-to-all(bf16[32,32,128]{2,1,0:T(8,128)(2,1)S(1)} %pool.1), channel_id=1, replica_groups=mesh['chip'=4,'core'=2,'mp'=4] {'chip','core','mp'}, dimensions={0} | all-to-all | bytes 524288 | tf_op jit(solution)/shard_map/all_to_all | solution.py:282
  32.6 0.0 copy-start
  32.6 5.8 %copy-done = bf16[8192,1024]{1,0:T(8,128)(2,1)S(1)} copy-done((bf16[8192,1024]{1,0:T(8,128)(2,1)S(1)}, bf16[8192,1024]{1,0:T(8,128)(2,1)}, u32[]{:S(2)}) %copy-start) | copy-done | bytes 16777240
  38.3 0.0 copy-start.3
  38.3 0.9 %copy-done.3 = bf16[512,256]{1,0:T(8,128)(2,1)S(1)} copy-done((bf16[512,256]{1,0:T(8,128)(2,1)S(1)}, bf16[512,256]{1,0:T(8,128)(2,1)}, u32[]{:S(2)}) %copy-start.3) | copy-done | bytes 262168
  39.3 2.5 %project.1 = (f32[96,256]{1,0:T(8,128)S(1)}, bf16[96,256]{1,0:T(8,128)(2,1)S(1)}) custom-call(bf16[32,32,128]{2,1,0:T(8,128)(2,1)S(1)} %all_to_all.10.got, bf16[512,256]{1,0:T(8,128)(2,1)S(1)} %copy-done.3, bf16[8192,1024]{1,0:T(8,128)(2,1)S(1)} %copy-done), custom_call_target="tpu_custom_call" | custom-call | tf_op jit(solution)/shard_map/project/pallas_call | solution.py:284
  41.8 0.4 collective-permute-start
  42.2 0.9 %collective-permute-done.other = bf16[96,256]{1,0:T(8,128)(2,1)S(1)} collective-permute-done((bf16[96,256]{1,0:T(8,128)(2,1)S(1)}, bf16[96,256]{1,0:T(8,128)(2,1)S(1)}, u32[]{:S(2)}, u32[]{:S(2)}) %collective-permute-start) | collective-permute-done | bytes 49184 | tf_op jit(solution)/shard_map/ppermute | solution.py:307
  43.1 0.0 copy-done.2
  43.1 0.2 rotate.1
  43.3 13.0 %all_to_all.11.parts = bf16[16,24,256]{2,1,0:T(8,128)(2,1)S(1)} all-to-all(bf16[16,24,256]{2,1,0:T(8,128)(2,1)S(1)} %rotate.1), channel_id=1, replica_groups=mesh['chip'=4,'core'=2,'mp'=4] {'chip','mp'}, dimensions={0} | all-to-all | bytes 393216 | tf_op jit(solution)/shard_map/all_to_all | solution.py:316
  56.3 0.7 %quantize.1 = (bf16[24,256]{1,0:T(8,128)(2,1)}, bf16[4,24]{1,0:T(4,128)(2,1)}) custom-call(bf16[16,24,256]{2,1,0:T(8,128)(2,1)S(1)} %all_to_all.11.parts), custom_call_target="tpu_custom_call" | custom-call | tf_op jit(solution)/shard_map/quantize/pallas_call | solution.py:317
Async XLA Ops:
  0.6 4.6 %copy-start.1 = (bf16[6,256,4096]{2,1,0:T(8,128)(2,1)S(1)}, bf16[6,256,4096]{2,1,0:T(8,128)(2,1)}, u32[]{:S(2)}) copy-start(bf16[6,256,4096]{2,1,0:T(8,128)(2,1)} %hidden.1) | copy-start | bytes 37748740
  5.2 0.9 %copy-start.4 = (s32[65536]{0:T(1024)S(1)}, s32[65536]{0:T(1024)}, u32[]{:S(2)}) copy-start(s32[65536]{0:T(1024)} %param.13) | copy-start | bytes 786436
  6.2 0.7 %copy-start.5 = (bf16[4096]{0:T(1024)(128)(2,1)S(1)}, bf16[4096]{0:T(1024)(128)(2,1)}, u32[]{:S(2)}) copy-start(bf16[4096]{0:T(1024)(128)(2,1)} %param.11) | copy-start | bytes 24580
  6.9 0.7 %copy-start.6 = (s32[6]{0:T(128)S(1)}, s32[6]{0:T(128)}, u32[]{:S(2)}) copy-start(s32[6]{0:T(128)} %lens.1) | copy-start | bytes 76
  7.5 0.7 %copy-start.7 = (s32[24]{0:T(128)S(1)}, s32[24]{0:T(128)}, u32[]{:S(2)}) copy-start(s32[24]{0:T(128)} %ids.1) | copy-start | bytes 292
  8.2 34.9 %copy-start.2 = (bf16[256,1024]{1,0:T(8,128)(2,1)S(1)}, bf16[256,1024]{1,0:T(8,128)(2,1)}, u32[]{:S(2)}) copy-start(bf16[256,1024]{1,0:T(8,128)(2,1)} %rotation.1) | copy-start | bytes 1572868
  32.6 5.8 %copy-start = (bf16[8192,1024]{1,0:T(8,128)(2,1)S(1)}, bf16[8192,1024]{1,0:T(8,128)(2,1)}, u32[]{:S(2)}) copy-start(bf16[8192,1024]{1,0:T(8,128)(2,1)} %cents.1) | copy-start | bytes 50331652
  38.3 0.9 %copy-start.3 = (bf16[512,256]{1,0:T(8,128)(2,1)S(1)}, bf16[512,256]{1,0:T(8,128)(2,1)}, u32[]{:S(2)}) copy-start(bf16[512,256]{1,0:T(8,128)(2,1)} %head.1) | copy-start | bytes 786436
  41.8 1.3 %collective-permute-start = (bf16[96,256]{1,0:T(8,128)(2,1)S(1)}, bf16[96,256]{1,0:T(8,128)(2,1)S(1)}, u32[]{:S(2)}, u32[]{:S(2)}) collective-permute-start(bf16[96,256]{1,0:T(8,128)(2,1)S(1)} %get-tuple-element.7), channel_id=1, source_target_pairs={{0,4},{4,0},{1,5},{5,1},{2,6},{6,2},{3,7},{7,3},{8,12},{12,8},{9,1... | collective-permute-start | bytes 147464 | tf_op jit(solution)/shard_map/ppermute | solution.py:307
where the time goes:
time: 57.3 us; the launch traced here: 57 us
  blocking collectives  31.9 us (56%)
  local copies, waits for them, and re-layouts  14.2 us (25%)
  Pallas kernels  8.93 us (16%)
  waiting for transfers between devices  0.89 us (2%)
  between operations  0.67 us (1%)
    all_to_all x1, blocking collectives, per_device(): got = lax.all_to_all(blocks, ('chip', 'core', 'mp'), 0, 0, tiled=True)  18.9 us
    unnamed x16, local copies, waits for them, and re-layouts  14.2 us
    all_to_all x1, blocking collectives, per_device(): parts = lax.all_to_all(parts, ('chip', 'mp'), 0, 0, tiled=True)  13 us
    pallas_call x1, Pallas kernels, per_device(): pl.pallas_call(functools.partial(pool_kernel, owners=owners, peers=peers,...  5.49 us
    pallas_call x1, Pallas kernels, per_device(): pl.pallas_call(functools.partial(project_kernel, owners=owners, peers=pee...  2.49 us
  transfers between devices with their start and end apart: 1, of which 1 were waited for; matrix products, arithmetic and copies ran while one was open for 0% of the time, Pallas kernels for 0%

commit v1 on v0

--- a/solution.py
+++ b/solution.py
@@ -23,9 +23,13 @@
     return pltpu.with_memory_space_constraint(x, pltpu.VMEM)
 
 
+def far(x):
+    return pltpu.with_memory_space_constraint(x, pltpu.HBM)
+
+
 def pool_kernel(
-    lens, ids, hidden, slots, gain, out, buf, weight, acc, slot_rows, items, counts, sems, slot_sem,
-    *, owners, peers, lists_own, capacity, lead,
+    lens, ids, hidden, slots, gain, head, out, head_out, buf, weight, acc, slot_rows, items, counts,
+    sems, slot_sem, head_sem, *, owners, peers, lists_own, capacity, lead,
 ):
     passes, length, width = hidden.shape
     group = ids.shape[0]
@@ -56,6 +60,8 @@
             count = count + needed.astype(jnp.int32)
     for g in range(group):
         slot_copy(g).start()
+    head_copy = pltpu.make_async_copy(head, head_out, head_sem)
+    head_copy.start()
     for o in range(owners):
         counts[o] = 0
 
@@ -115,6 +121,7 @@
     lax.fori_loop(0, count - 1, body, 0)
     add(count - 1)
 
+    head_copy.wait()
     for g in range(group):
         slot_copy(g).wait()
     owner_row = lax.broadcasted_iota(jnp.int32, (lead, LANES), 0)
@@ -259,13 +266,16 @@
     vmem = pl.BlockSpec(memory_space=pltpu.VMEM)
     smem = pl.BlockSpec(memory_space=pltpu.SMEM)
     hbm = pl.BlockSpec(memory_space=pl.ANY)
-    blocks = pl.pallas_call(
+    blocks, head = pl.pallas_call(
         functools.partial(
             pool_kernel, owners=owners, peers=peers, lists_own=lists_own, capacity=capacity, lead=lead
         ),
-        out_shape=pltpu.VMEM((owners * peers, per * rows, LANES), BF16),
-        in_specs=[smem, smem, hbm, hbm, vmem],
-        out_specs=vmem,
+        out_shape=(
+            pltpu.VMEM((owners * peers, per * rows, LANES), BF16),
+            pltpu.VMEM(head.shape, BF16),
+        ),
+        in_specs=[smem, smem, hbm, hbm, vmem, hbm],
+        out_specs=(vmem, vmem),
         scratch_shapes=[
             pltpu.VMEM((passes * steps, STEP, width), BF16),
             pltpu.VMEM((2, STEP, LANES), F32),
@@ -275,10 +285,14 @@
             pltpu.SMEM((owners,), jnp.int32),
             pltpu.SemaphoreType.DMA((passes * steps,)),
             pltpu.SemaphoreType.DMA,
+            pltpu.SemaphoreType.DMA,
         ],
         compiler_params=pltpu.CompilerParams(vmem_limit_bytes=hidden.size * 2 + 6 * 2**20),
         name="pool",
-    )(lengths, list_ids, hidden, list_slot.reshape(-1, LANES), gain.reshape(-1, LANES))
+    )(
+        far(lengths), far(list_ids), far(hidden), far(list_slot.reshape(-1, LANES)),
+        far(gain.reshape(-1, LANES)), far(head),
+    )
     got = lax.all_to_all(blocks, ("chip", "core", "mp"), 0, 0, tiled=True)
     half = owners // CORES * group
     own, other = pl.pallas_call(
@@ -303,7 +317,7 @@
         ],
         compiler_params=pltpu.CompilerParams(vmem_limit_bytes=8 * 2**20),
         name="project",
-    )(near(got), near(head), centroids)
+    )(near(got), near(head), far(centroids))
     other = lax.ppermute(other, "core", [(c, (c + 1) % CORES) for c in range(CORES)])
     parts = pl.pallas_call(
         functools.partial(rotate_kernel, peers=peers),

time: 57.3 us -> 44.2 us (0.77)
  local copies, waits for them, and re-layouts: 14.2 us -> 0.01 us
  Pallas kernels: 8.93 us -> 12.2 us
  blocking collectives: 31.9 us -> 29.6 us
    unnamed x16 -> x2, local copies, waits for them, and re-layouts: 14.2 us -> 0.01 us
    pallas_call x1, Pallas kernels: 5.49 us -> 7.99 us  [per_device(): pl.pallas_call(functools.partial(pool_kernel, owners=owners, peers=peers,...]
    all_to_all x1, blocking collectives: 18.9 us -> 16.4 us  [per_device(): got = lax.all_to_all(blocks, ('chip', 'core', 'mp'), 0, 0, tiled=True)]
    pallas_call x1, Pallas kernels: 2.49 us -> 3.28 us  [per_device(): pl.pallas_call(functools.partial(project_kernel, owners=owners, peers=pee...]
where the time goes in v1:
time: 44.2 us; the launch traced here: 43.9 us
  blocking collectives  29.6 us (67%)
  Pallas kernels  12.2 us (28%)
  waiting for transfers between devices  0.88 us (2%)
  between operations  0.66 us (1%)
  starting transfers between devices  0.52 us (1%)
    all_to_all x1, blocking collectives, per_device(): got = lax.all_to_all(blocks, ('chip', 'core', 'mp'), 0, 0, tiled=True)  16.4 us
    all_to_all x1, blocking collectives, per_device(): parts = lax.all_to_all(parts, ('chip', 'mp'), 0, 0, tiled=True)  13.1 us
    pallas_call x1, Pallas kernels, per_device(): pl.pallas_call(functools.partial(pool_kernel, owners=owners, peers=peers,...  7.99 us
    pallas_call x1, Pallas kernels, per_device(): pl.pallas_call(functools.partial(project_kernel, owners=owners, peers=pee...  3.28 us
  transfers between devices with their start and end apart: 1, of which 1 were waited for; matrix products, arithmetic and copies ran while one was open for 0% of the time, Pallas kernels for 0%

profile of v1, /device:TPU:0, one launch (start us, length us, event | category | flops | bytes accessed | tf_op | source)
XLA Modules:
  0.0 43.9 jit_solution(6801211752004383788)
XLA Ops:
  0.6 0.0 copy-start
  0.6 8.0 %pool.1 = (bf16[32,32,128]{2,1,0:T(8,128)(2,1)S(1)}, bf16[512,256]{1,0:T(8,128)(2,1)S(1)}) custom-call(s32[6]{0:T(128)} %lens.1, s32[24]{0:T(128)} %ids.1, bf16[6,256,4096]{2,1,0:T(8,128)(2,1)} %hidden.1, s32[512,128]{1,0:T(8,128)} %bitcast.3, bf16[32,128]{1,0:T(8,128)(2,1)} %bitcast.4, bf16[512,256]{1,0:T(8,128)(2,1)} %head.1), custom_call_target="tpu_custom_call" | custom-call | tf_op jit(solution)/shard_map/pool/pallas_call | solution.py:269
  8.6 16.4 %all_to_all.10.got = bf16[32,32,128]{2,1,0:T(8,128)(2,1)S(1)} all-to-all(bf16[32,32,128]{2,1,0:T(8,128)(2,1)S(1)} %get-tuple-element.8), channel_id=1, replica_groups=mesh['chip'=4,'core'=2,'mp'=4] {'chip','core','mp'}, dimensions={0} | all-to-all | bytes 524288 | tf_op jit(solution)/shard_map/all_to_all | solution.py:296
  25.1 3.3 %project.1 = (f32[96,256]{1,0:T(8,128)S(1)}, bf16[96,256]{1,0:T(8,128)(2,1)S(1)}) custom-call(bf16[32,32,128]{2,1,0:T(8,128)(2,1)S(1)} %all_to_all.10.got, bf16[512,256]{1,0:T(8,128)(2,1)S(1)} %get-tuple-element.9.head, bf16[8192,1024]{1,0:T(8,128)(2,1)} %cents.1), custom_call_target="tpu_custom_call" | custom-call | tf_op jit(solution)/shard_map/project/pallas_call | solution.py:298
  28.4 0.5 %collective-permute-start = (bf16[96,256]{1,0:T(8,128)(2,1)S(1)}, bf16[96,256]{1,0:T(8,128)(2,1)S(1)}, u32[]{:S(2)}, u32[]{:S(2)}) collective-permute-start(bf16[96,256]{1,0:T(8,128)(2,1)S(1)} %get-tuple-element.11), channel_id=1, source_target_pairs={{0,4},{4,0},{1,5},{5,1},{2,6},{6,2},{3,7},{7,3},{8,12},{12,8},{9,1... | collective-permute-start | bytes 147464 | tf_op jit(solution)/shard_map/ppermute | solution.py:321
  28.9 0.9 %collective-permute-done.other = bf16[96,256]{1,0:T(8,128)(2,1)S(1)} collective-permute-done((bf16[96,256]{1,0:T(8,128)(2,1)S(1)}, bf16[96,256]{1,0:T(8,128)(2,1)S(1)}, u32[]{:S(2)}, u32[]{:S(2)}) %collective-permute-start) | collective-permute-done | bytes 49184 | tf_op jit(solution)/shard_map/ppermute | solution.py:321
  29.8 0.0 copy-done
  29.8 0.2 rotate.1
  30.0 13.1 %all_to_all.11.parts = bf16[16,24,256]{2,1,0:T(8,128)(2,1)S(1)} all-to-all(bf16[16,24,256]{2,1,0:T(8,128)(2,1)S(1)} %rotate.1), channel_id=1, replica_groups=mesh['chip'=4,'core'=2,'mp'=4] {'chip','mp'}, dimensions={0} | all-to-all | bytes 393216 | tf_op jit(solution)/shard_map/all_to_all | solution.py:330
  43.1 0.7 %quantize.1 = (bf16[24,256]{1,0:T(8,128)(2,1)}, bf16[4,24]{1,0:T(4,128)(2,1)}) custom-call(bf16[16,24,256]{2,1,0:T(8,128)(2,1)S(1)} %all_to_all.11.parts), custom_call_target="tpu_custom_call" | custom-call | tf_op jit(solution)/shard_map/quantize/pallas_call | solution.py:331
Async XLA Ops:
  0.6 29.2 %copy-start = (bf16[256,1024]{1,0:T(8,128)(2,1)S(1)}, bf16[256,1024]{1,0:T(8,128)(2,1)}, u32[]{:S(2)}) copy-start(bf16[256,1024]{1,0:T(8,128)(2,1)} %rotation.1) | copy-start | bytes 1572868
  28.4 1.4 %collective-permute-start = (bf16[96,256]{1,0:T(8,128)(2,1)S(1)}, bf16[96,256]{1,0:T(8,128)(2,1)S(1)}, u32[]{:S(2)}, u32[]{:S(2)}) collective-permute-start(bf16[96,256]{1,0:T(8,128)(2,1)S(1)} %get-tuple-element.11), channel_id=1, source_target_pairs={{0,4},{4,0},{1,5},{5,1},{2,6},{6,2},{3,7},{7,3},{8,12},{12,8},{9,1... | collective-permute-start | bytes 147464 | tf_op jit(solution)/shard_map/ppermute | solution.py:321

commit v2 on v0

v2 whole, which is shorter than its diff:
```python
import functools

import jax
import jax.numpy as jnp
from jax import lax
from jax.experimental import pallas as pl
from jax.experimental.pallas import tpu as pltpu
from jax.sharding import Mesh
from jax.sharding import PartitionSpec as P

BLOCK = 64
LANES = 128
SUB = 8
DIGIT = 256
CORES = 2
STEP = 64

F32 = jnp.float32
BF16 = jnp.bfloat16


def near(x):
    return pltpu.with_memory_space_constraint(x, pltpu.VMEM)


def far(x):
    return pltpu.with_memory_space_constraint(x, pltpu.HBM)


def pool_kernel(
    lens_hbm, ids_hbm, hidden, slots, gain_hbm, head, out, head_out, buf, weight, acc, slot_rows, gain,
    lens, ids, items, sems, slot_sem, side_sems, *, owners, peers, lists_own, capacity,
):
    passes, length, width = hidden.shape
    group = ids.shape[0]
    steps = length // STEP
    tiles = width // LANES
    per = tiles // owners
    rows = out.shape[1] // per

    def chunk_copy(p, c):
        return pltpu.make_async_copy(
            hidden.at[p, pl.ds(c * STEP, STEP)], buf.at[p * steps + c], sems.at[p * steps + c]
        )

    def slot_copy(g):
        return pltpu.make_async_copy(
            slots.at[pl.ds(lax.div(ids[g], LANES), 1)], slot_rows.at[pl.ds(g, 1)], slot_sem
        )

    side = [
        pltpu.make_async_copy(source, target, side_sems.at[n])
        for n, (source, target) in enumerate(
            ((lens_hbm, lens), (ids_hbm, ids), (gain_hbm, gain), (head, head_out))
        )
    ]
    side[0].start()
    side[1].start()
    for p in range(passes):
        chunk_copy(p, 0).start()
        items[p] = p * steps
    side[0].wait()
    count = jnp.int32(passes)
    for c in range(1, steps):
        for p in range(passes):
            needed = lens[p] > c * STEP

            @pl.when(needed)
            def _():
                chunk_copy(p, c).start()
                items[count] = p * steps + c

            count = count + needed.astype(jnp.int32)
    side[1].wait()
    for g in range(group):
        slot_copy(g).start()
    side[2].start()
    side[3].start()

    def zero(p, _):
        acc[p] = jnp.zeros((SUB, width), F32)
        return 0

    lax.fori_loop(0, passes, zero, 0)

    def arrive(k):
        item = items[k]
        pltpu.make_async_copy(
            hidden.at[0, pl.ds(0, STEP)], buf.at[item], sems.at[item]
        ).wait()

    def weigh(k):
        item = items[k]
        p = lax.div(item, steps)
        start = lax.rem(item, steps) * STEP
        size = lens[p]
        for s in range(0, STEP, SUB):
            x = buf[item, s : s + SUB, :]
            x = x * x
            x = (x[:, : width // 2] + x[:, width // 2 :]).astype(F32)
            total = x[:, :LANES]
            for t in range(LANES, width // 2, LANES):
                total = total + x[:, t : t + LANES]
            square = jnp.sum(total, axis=1, keepdims=True)
            token = lax.broadcasted_iota(jnp.int32, (SUB, 1), 0) + (start + s)
            value = jnp.where(token < size, lax.rsqrt(square * (1.0 / width) + 1e-05), 0.0)
            weight[lax.rem(k, 2), s : s + SUB, :] = jnp.broadcast_to(value, (SUB, LANES))

    def add(k):
        item = items[k]
        p = lax.div(item, steps)
        w = weight[lax.rem(k, 2)]
        for t in range(tiles):
            x = buf[item, :, t * LANES : (t + 1) * LANES].astype(F32) * w
            part = x[0:SUB]
            for s in range(SUB, STEP, SUB):
                part = part + x[s : s + SUB]
            acc[p, :, t * LANES : (t + 1) * LANES] += part

    arrive(0)
    weigh(jnp.int32(0))

    def body(k, _):
        arrive(k + 1)
        add(k)
        weigh(k + 1)
        return 0

    lax.fori_loop(0, count - 1, body, 0)
    for n in (2, 3):
        side[n].wait()
    for g in range(group):
        slot_copy(g).wait()
    add(count - 1)

    shape = (-(-group // SUB) * SUB, LANES)
    sub = lax.broadcasted_iota(jnp.int32, (SUB, LANES), 0)
    blocks = []
    for start in range(0, shape[0], SUB):
        block = jnp.zeros((SUB, LANES), jnp.int32)
        for g in range(start, min(start + SUB, group)):
            block = jnp.where(sub == g - start, lax.rem(ids[g], LANES), block)
        blocks.append(block)
    column = jnp.concatenate(blocks, axis=0)
    line = lax.broadcasted_iota(jnp.int32, shape, 0)
    lane = lax.broadcasted_iota(jnp.int32, shape, 1)
    picked = jnp.where((lane == column) & (line < group), slot_rows[...], 0).astype(F32)
    slot = jnp.sum(picked, axis=1, keepdims=True).astype(jnp.int32)
    slot = jnp.broadcast_to(slot, shape)
    owner = lax.div(slot, lists_own)
    local = slot - owner * lists_own
    high = lax.div(local, DIGIT)
    low = local - high * DIGIT
    owner_line = jnp.sum(jnp.where(line == lane, owner.astype(F32), 0.0), axis=0, keepdims=True)
    earlier = (jnp.broadcast_to(owner_line, shape) == owner.astype(F32)) & (lane < line)
    rank = jnp.sum(jnp.where(earlier, 1.0, 0.0), axis=1, keepdims=True).astype(jnp.int32)
    rank = jnp.broadcast_to(rank, shape)
    peer = jnp.zeros(shape, jnp.int32)
    for j in range(1, peers):
        peer = peer + (line >= j * passes).astype(jnp.int32)
    place = line + peer * (rows - passes) + 1
    entry = jnp.where(lane == rank, high, 0)
    entry = jnp.where(lane == rank + capacity, low, entry)
    entry = jnp.where(lane == rank + 2 * capacity, place, entry)
    entry = jnp.where((rank < capacity) & (line < group), entry, 0).astype(F32)

    inverse = jnp.zeros((SUB, LANES), F32)
    for p in range(passes):
        inverse = jnp.where(sub == p, lens[p].astype(F32), inverse)
    inverse = jnp.where(sub < passes, 1.0 / jnp.maximum(inverse, 1.0), 0.0)
    for o in range(owners):
        info = jnp.sum(jnp.where(owner == o, entry, 0.0), axis=0, keepdims=True)
        for q in range(per):
            t = o * per + q
            cols = slice(t * LANES, (t + 1) * LANES)
            parts = [acc[p, :, cols] if p < passes else None for p in range(SUB)]
            bit = SUB // 2
            while bit:
                merged = []
                for n in range(bit):
                    a, b = parts[n], parts[n + bit]
                    if a is None:
                        merged.append(None)
                    elif b is None:
                        merged.append(jnp.where((sub & bit) == 0, a + pltpu.roll(a, SUB - bit, 0), 0.0))
                    else:
                        first = jnp.where((sub & bit) == 0, a, b)
                        second = jnp.where((sub & bit) == 0, b, a)
                        if bit * 2 == SUB:
                            merged.append(first + pltpu.roll(second, bit, 0))
                        else:
                            up = pltpu.roll(second, SUB - bit, 0)
                            down = pltpu.roll(second, bit, 0)
                            merged.append(first + jnp.where((sub & bit) == 0, up, down))
                parts = merged
                bit //= 2
            tile = parts[0] * gain[t : t + 1].astype(F32) * inverse
            if q == 0:
                tile = jnp.where(sub == passes, jnp.broadcast_to(info, (SUB, LANES)), tile)
            tile = tile.astype(BF16)
            for j in range(peers):
                out[o * peers + j, q * rows : (q + 1) * rows, :] = tile


def project_kernel(
    got, head, cents, own, other, info_v, info_s, acc, rows_in, packed, info_sem, row_sems,
    *, owners, peers, passes, capacity,
):
    rows = SUB
    width = head.shape[1]
    lists_own = cents.shape[0]
    per = got.shape[1] // rows
    wide = peers * rows
    col = pl.multiple_of(lax.axis_index("mp") * width, LANES)
    for o in range(owners):
        line = got[o * peers, 0:rows, :].astype(F32)[passes : passes + 1]
        info_v[o : o + 1, :] = line.astype(jnp.int32)
    info_copy = pltpu.make_async_copy(info_v, info_s, info_sem)
    info_copy.start()
    info_copy.wait()
    entries = [(o, k) for o in range(owners) for k in range(capacity)]

    def row_copy(n, first):
        return pltpu.make_async_copy(
            cents.at[pl.ds(first, SUB), pl.ds(col, width)], rows_in.at[n], row_sems.at[n]
        )

    which = []
    for n, (o, k) in enumerate(entries):
        row = jnp.clip(info_s[o, k] * DIGIT + info_s[o, capacity + k], 0, lists_own - 1)
        first = lax.div(row, SUB) * SUB
        row_copy(n, pl.multiple_of(first, SUB)).start()
        which.append(row - first)
    total = None
    for q in range(per):
        x = got[:, q * rows : (q + 1) * rows, :].reshape(owners * peers * rows, LANES)
        y = jnp.dot(x, head[q * LANES : (q + 1) * LANES, :], preferred_element_type=F32)
        total = y if total is None else total + y
    lane = lax.broadcasted_iota(jnp.int32, (1, LANES), 1)
    share = LANES // SUB
    for n in range(len(entries)):
        row_copy(n, 0).wait()
    for start in range(0, len(entries), share):
        part = entries[start : start + share]
        target = jnp.full((1, LANES), -1, jnp.int32)
        for m, (o, k) in enumerate(part):
            place = info_s[o, 2 * capacity + k]
            at = jnp.where((place > 0) & (place <= wide), o * wide + place - 1, -1)
            target = jnp.where(lane == m * SUB + which[start + m], at, target)
        depth = len(part) * SUB
        spots = lax.broadcasted_iota(jnp.int32, (owners * wide, LANES), 0)
        chosen = jnp.where(spots == target, 1.0, 0.0).astype(BF16)[:, :depth]
        lines = rows_in[start : start + len(part)].reshape(depth, width)
        total = total - jnp.dot(chosen, lines, preferred_element_type=F32)
    acc[...] = total.reshape(owners, wide, width)
    core = lax.axis_index("core")
    group = peers * passes
    for side in range(CORES):
        for c in range(owners // CORES):
            x = acc[c * CORES + (core if side == 0 else 1 - core)]
            for j in range(peers):
                at = c * group + j * passes
                packed[side, at : at + passes, :] = x[j * rows : j * rows + passes]
    own[...] = packed[0]
    other[...] = packed[1].astype(BF16)


def rotate_kernel(own, other, rotation, out, *, peers):
    group = out.shape[1]
    width = out.shape[2]
    resid = (own[...] + other[...].astype(F32)).astype(BF16)
    for j in range(peers):
        y = jnp.dot(
            resid, rotation[:, j * width : (j + 1) * width], preferred_element_type=F32
        ).astype(BF16)
        for c in range(resid.shape[0] // group):
            out[c * peers + j] = y[c * group : (c + 1) * group]


def quantize_kernel(parts, codes, scales):
    total = parts[0].astype(F32)
    for s in range(1, parts.shape[0]):
        total = total + parts[s].astype(F32)
    group, width = total.shape
    lane = lax.broadcasted_iota(jnp.int32, (group, LANES), 1)
    table = jnp.zeros((group, LANES), F32)
    for t in range(width // LANES):
        x = total[:, t * LANES : (t + 1) * LANES]
        size = jnp.abs(x)
        spread = jnp.zeros((group, LANES), F32)
        for b in range(LANES // BLOCK):
            inside = (lane >= b * BLOCK) & (lane < (b + 1) * BLOCK)
            top = jnp.max(jnp.where(inside, size, 0.0), axis=1, keepdims=True) + 1e-06
            spread = jnp.where(inside, top, spread)
            table = jnp.where(lane == t * (LANES // BLOCK) + b, top, table)
        codes[:, t * LANES : (t + 1) * LANES] = (x / spread).astype(BF16)
    scales[...] = table.T[: scales.shape[0]].astype(BF16)


def pool_call(lengths, list_ids, hidden, list_slot, gain, head, *, owners, peers, lists_own):
    passes, length, width = hidden.shape
    assert passes < SUB and length % STEP == 0
    group = list_ids.shape[0]
    capacity = max(2, 2 * group // owners)
    per = width // LANES // owners
    steps = length // STEP
    padded = -(-group // SUB) * SUB
    vmem = pl.BlockSpec(memory_space=pltpu.VMEM)
    hbm = pl.BlockSpec(memory_space=pl.ANY)
    return pl.pallas_call(
        functools.partial(
            pool_kernel, owners=owners, peers=peers, lists_own=lists_own, capacity=capacity
        ),
        out_shape=(
            pltpu.VMEM((owners * peers, per * SUB, LANES), BF16),
            pltpu.VMEM(head.shape, BF16),
        ),
        in_specs=[hbm] * 6,
        out_specs=(vmem, vmem),
        scratch_shapes=[
            pltpu.VMEM((passes * steps, STEP, width), BF16),
            pltpu.VMEM((2, STEP, LANES), F32),
            pltpu.VMEM((passes, SUB, width), F32),
            pltpu.VMEM((padded, LANES), jnp.int32),
            pltpu.VMEM((width // LANES, LANES), BF16),
            pltpu.SMEM((passes,), jnp.int32),
            pltpu.SMEM((group,), jnp.int32),
            pltpu.SMEM((passes * steps,), jnp.int32),
            pltpu.SemaphoreType.DMA((passes * steps,)),
            pltpu.SemaphoreType.DMA,
            pltpu.SemaphoreType.DMA((4,)),
        ],
        compiler_params=pltpu.CompilerParams(vmem_limit_bytes=hidden.size * 2 + 6 * 2**20),
        name="pool",
    )(
        far(lengths), far(list_ids), far(hidden), far(list_slot.reshape(-1, LANES)),
        far(gain.reshape(-1, LANES)), far(head),
    )


def per_device(hidden, lengths, list_ids, gain, head, list_slot, centroids, rotation):
    passes, length, width = hidden.shape
    owners = lax.axis_size("chip") * lax.axis_size("core")
    peers = lax.axis_size("mp")
    group = list_ids.shape[0]
    lists_own = centroids.shape[0]
    capacity = max(2, 2 * group // owners)
    cols = head.shape[1]
    lead = -(-owners // SUB) * SUB
    vmem = pl.BlockSpec(memory_space=pltpu.VMEM)
    hbm = pl.BlockSpec(memory_space=pl.ANY)
    blocks, head = pool_call(
        lengths, list_ids, hidden, list_slot, gain, head,
        owners=owners, peers=peers, lists_own=lists_own,
    )
    got = lax.all_to_all(blocks, ("chip", "core", "mp"), 0, 0, tiled=True)
    half = owners // CORES * group
    own, other = pl.pallas_call(
        functools.partial(
            project_kernel, owners=owners, peers=peers, passes=passes, capacity=capacity
        ),
        out_shape=(
            pltpu.VMEM((half, cols), F32),
            pltpu.VMEM((half, cols), BF16),
        ),
        in_specs=[vmem, vmem, hbm],
        out_specs=(vmem, vmem),
        scratch_shapes=[
            pltpu.VMEM((lead, LANES), jnp.int32),
            pltpu.SMEM((lead, LANES), jnp.int32),
            pltpu.VMEM((owners, peers * SUB, cols), F32),
            pltpu.VMEM((owners * capacity, SUB, cols), BF16),
            pltpu.VMEM((CORES, half, cols), F32),
            pltpu.SemaphoreType.DMA,
            pltpu.SemaphoreType.DMA((owners * capacity,)),
        ],
        compiler_params=pltpu.CompilerParams(vmem_limit_bytes=8 * 2**20),
        name="project",
    )(near(got), near(head), far(centroids))
    other = lax.ppermute(other, "core", [(c, (c + 1) % CORES) for c in range(CORES)])
    parts = pl.pallas_call(
        functools.partial(rotate_kernel, peers=peers),
        out_shape=pltpu.VMEM((owners // CORES * peers, group, cols), BF16),
        in_specs=[vmem, vmem, vmem],
        out_specs=vmem,
        compiler_params=pltpu.CompilerParams(vmem_limit_bytes=8 * 2**20),
        name="rotate",
    )(near(own), near(other), near(rotation))
    parts = lax.all_to_all(parts, ("chip", "mp"), 0, 0, tiled=True)
    codes, scales = pl.pallas_call(
        quantize_kernel,
        out_shape=(
            jax.ShapeDtypeStruct((group, cols), BF16),
            jax.ShapeDtypeStruct((cols // BLOCK, group), BF16),
        ),
        in_specs=[vmem],
        out_specs=(vmem, vmem),
        compiler_params=pltpu.CompilerParams(vmem_limit_bytes=8 * 2**20),
        name="quantize",
    )(near(parts))
    return codes, scales.T


def solution(mesh):
    dp, mp = mesh.shape["dp"], mesh.shape["mp"]
    split = Mesh(mesh.devices.reshape(dp // CORES, CORES, mp), ("chip", "core", "mp"))
    rows = ("chip", "core")
    in_specs = (
        P(("chip", "core", "mp"), None, None),
        P(("chip", "core", "mp")),
        P(rows),
        P(),
        P(rows, "mp"),
        P(),
        P(rows, None),
        P("mp", None),
    )
    out_specs = (P(rows, "mp"), P(rows, "mp"))
    return jax.shard_map(
        per_device, mesh=split, in_specs=in_specs, out_specs=out_specs, check_vma=False
    )
```

time: 57.3 us -> 41.5 us (0.72)
  local copies, waits for them, and re-layouts: 14.2 us -> 0.01 us
  blocking collectives: 31.9 us -> 30.1 us
  starting transfers between devices: 0.4 us -> 1.02 us
  Pallas kernels: 8.93 us -> 8.34 us
    unnamed x16 -> x2, local copies, waits for them, and re-layouts: 14.2 us -> 0.01 us
    all_to_all x1, blocking collectives: 18.9 us -> 17 us  [per_device(): got = lax.all_to_all(blocks, ('chip', 'core', 'mp'), 0, 0, tiled=True)]
    pallas_call x1, Pallas kernels: 5.49 us -> 4.71 us  [pool_call(): pl.pallas_call(functools.partial(pool_kernel, owners=owners, peers=peers,...]
    ppermute x1, starting transfers between devices: 0.4 us -> 1.02 us  [per_device(): lax.ppermute(other, 'core', [(c, (c + 1) % CORES) for c in range(CORES)])]
where the time goes in v2:
time: 41.5 us; the launch traced here: 41 us
  blocking collectives  30.1 us (73%)
  Pallas kernels  8.34 us (20%)
  starting transfers between devices  1.02 us (2%)
  waiting for transfers between devices  0.88 us (2%)
  between operations  0.66 us (2%)
    all_to_all x1, blocking collectives, per_device(): got = lax.all_to_all(blocks, ('chip', 'core', 'mp'), 0, 0, tiled=True)  17 us
    all_to_all x1, blocking collectives, per_device(): parts = lax.all_to_all(parts, ('chip', 'mp'), 0, 0, tiled=True)  13.1 us
    pallas_call x1, Pallas kernels, pool_call(): pl.pallas_call(functools.partial(pool_kernel, owners=owners, peers=peers,...  4.71 us
    pallas_call x1, Pallas kernels, per_device(): pl.pallas_call(functools.partial(project_kernel, owners=owners, peers=pee...  2.67 us
    ppermute x1, starting transfers between devices, per_device(): lax.ppermute(other, 'core', [(c, (c + 1) % CORES) for c in range(CORES)])  1.02 us
    ppermute x1, waiting for transfers between devices, per_device(): lax.ppermute(other, 'core', [(c, (c + 1) % CORES) for c in range(CORES)])  0.88 us
  transfers between devices with their start and end apart: 1, of which 1 were waited for; matrix products, arithmetic and copies ran while one was open for 0% of the time, Pallas kernels for 0%

profile of v2, /device:TPU:0, one launch (start us, length us, event | category | flops | bytes accessed | tf_op | source)
XLA Modules:
  0.0 41.0 jit_solution(12700564563401024691)
XLA Ops:
  0.6 0.0 copy-start
  0.6 4.7 %pool.1 = (bf16[32,32,128]{2,1,0:T(8,128)(2,1)S(1)}, bf16[512,256]{1,0:T(8,128)(2,1)S(1)}) custom-call(s32[6]{0:T(128)} %lens_hbm.1, s32[24]{0:T(128)} %ids_hbm.1, bf16[6,256,4096]{2,1,0:T(8,128)(2,1)} %hidden.1, s32[512,128]{1,0:T(8,128)} %bitcast.3, bf16[32,128]{1,0:T(8,128)(2,1)} %bitcast.4, bf16[512,256]{1,0:T(8,128)(2,1)} %head.1), custom_call_target="tpu_custom_call" | custom-call | tf_op jit(solution)/shard_map/pool/pallas_call | solution.py:310
  5.4 17.0 %all_to_all.10.got = bf16[32,32,128]{2,1,0:T(8,128)(2,1)S(1)} all-to-all(bf16[32,32,128]{2,1,0:T(8,128)(2,1)S(1)} %get-tuple-element.8), channel_id=1, replica_groups=mesh['chip'=4,'core'=2,'mp'=4] {'chip','core','mp'}, dimensions={0} | all-to-all | bytes 524288 | tf_op jit(solution)/shard_map/all_to_all | solution.py:356
  22.4 2.7 %project.1 = (f32[96,256]{1,0:T(8,128)S(1)}, bf16[96,256]{1,0:T(8,128)(2,1)S(1)}) custom-call(bf16[32,32,128]{2,1,0:T(8,128)(2,1)S(1)} %all_to_all.10.got, bf16[512,256]{1,0:T(8,128)(2,1)S(1)} %get-tuple-element.9.head, bf16[8192,1024]{1,0:T(8,128)(2,1)} %cents.1), custom_call_target="tpu_custom_call" | custom-call | tf_op jit(solution)/shard_map/project/pallas_call | solution.py:358
  25.0 1.0 %collective-permute-start = (bf16[96,256]{1,0:T(8,128)(2,1)S(1)}, bf16[96,256]{1,0:T(8,128)(2,1)S(1)}, u32[]{:S(2)}, u32[]{:S(2)}) collective-permute-start(bf16[96,256]{1,0:T(8,128)(2,1)S(1)} %get-tuple-element.11), channel_id=1, source_target_pairs={{0,4},{4,0},{1,5},{5,1},{2,6},{6,2},{3,7},{7,3},{8,12},{12,8},{9,1... | collective-permute-start | bytes 147464 | tf_op jit(solution)/shard_map/ppermute | solution.py:380
  26.1 0.9 %collective-permute-done.other = bf16[96,256]{1,0:T(8,128)(2,1)S(1)} collective-permute-done((bf16[96,256]{1,0:T(8,128)(2,1)S(1)}, bf16[96,256]{1,0:T(8,128)(2,1)S(1)}, u32[]{:S(2)}, u32[]{:S(2)}) %collective-permute-start) | collective-permute-done | bytes 49184 | tf_op jit(solution)/shard_map/ppermute | solution.py:380
  26.9 0.0 copy-done
  26.9 0.2 rotate.1
  27.2 13.1 %all_to_all.11.parts = bf16[16,24,256]{2,1,0:T(8,128)(2,1)S(1)} all-to-all(bf16[16,24,256]{2,1,0:T(8,128)(2,1)S(1)} %rotate.1), channel_id=1, replica_groups=mesh['chip'=4,'core'=2,'mp'=4] {'chip','mp'}, dimensions={0} | all-to-all | bytes 393216 | tf_op jit(solution)/shard_map/all_to_all | solution.py:389
  40.3 0.7 %quantize.1 = (bf16[24,256]{1,0:T(8,128)(2,1)}, bf16[4,24]{1,0:T(4,128)(2,1)}) custom-call(bf16[16,24,256]{2,1,0:T(8,128)(2,1)S(1)} %all_to_all.11.parts), custom_call_target="tpu_custom_call" | custom-call | tf_op jit(solution)/shard_map/quantize/pallas_call | solution.py:390
Async XLA Ops:
  0.6 26.3 %copy-start = (bf16[256,1024]{1,0:T(8,128)(2,1)S(1)}, bf16[256,1024]{1,0:T(8,128)(2,1)}, u32[]{:S(2)}) copy-start(bf16[256,1024]{1,0:T(8,128)(2,1)} %rotation.1) | copy-start | bytes 1572868
  25.0 1.9 %collective-permute-start = (bf16[96,256]{1,0:T(8,128)(2,1)S(1)}, bf16[96,256]{1,0:T(8,128)(2,1)S(1)}, u32[]{:S(2)}, u32[]{:S(2)}) collective-permute-start(bf16[96,256]{1,0:T(8,128)(2,1)S(1)} %get-tuple-element.11), channel_id=1, source_target_pairs={{0,4},{4,0},{1,5},{5,1},{2,6},{6,2},{3,7},{7,3},{8,12},{12,8},{9,1... | collective-permute-start | bytes 147464 | tf_op jit(solution)/shard_map/ppermute | solution.py:380

commit v3 on v2

--- a/solution.py
+++ b/solution.py
@@ -104,18 +104,22 @@
             square = jnp.sum(total, axis=1, keepdims=True)
             token = lax.broadcasted_iota(jnp.int32, (SUB, 1), 0) + (start + s)
             value = jnp.where(token < size, lax.rsqrt(square * (1.0 / width) + 1e-05), 0.0)
-            weight[lax.rem(k, 2), s : s + SUB, :] = jnp.broadcast_to(value, (SUB, LANES))
+            weight[lax.rem(k, 2), s : s + SUB, :] = jnp.broadcast_to(value, (SUB, 2 * LANES)).astype(BF16)
 
     def add(k):
         item = items[k]
         p = lax.div(item, steps)
-        w = weight[lax.rem(k, 2)]
-        for t in range(tiles):
-            x = buf[item, :, t * LANES : (t + 1) * LANES].astype(F32) * w
-            part = x[0:SUB]
-            for s in range(SUB, STEP, SUB):
-                part = part + x[s : s + SUB]
-            acc[p, :, t * LANES : (t + 1) * LANES] += part
+        slot = lax.rem(k, 2)
+        pair = 2 * LANES
+        for t in range(0, width, pair):
+            total = None
+            for s in range(0, STEP, 2 * SUB):
+                x = buf[item, s : s + SUB, t : t + pair] * weight[slot, s : s + SUB, :]
+                e = s + SUB
+                x = x + buf[item, e : e + SUB, t : t + pair] * weight[slot, e : e + SUB, :]
+                x = x.astype(F32)
+                total = x if total is None else total + x
+            acc[p, :, t : t + pair] += total
 
     arrive(0)
     weigh(jnp.int32(0))
@@ -129,8 +133,9 @@
     lax.fori_loop(0, count - 1, body, 0)
     for n in (2, 3):
         side[n].wait()
-    for g in range(group):
-        slot_copy(g).wait()
+    pltpu.make_async_copy(
+        slots.at[pl.ds(0, group)], slot_rows.at[pl.ds(0, group)], slot_sem
+    ).wait()
     add(count - 1)
 
     shape = (-(-group // SUB) * SUB, LANES)
@@ -203,7 +208,7 @@
 
 
 def project_kernel(
-    got, head, cents, own, other, info_v, info_s, acc, rows_in, packed, info_sem, row_sems,
+    got, head, cents, own, other, info_v, info_s, acc, rows_in, packed, info_sem, row_sem,
     *, owners, peers, passes, capacity,
 ):
     rows = SUB
@@ -212,46 +217,50 @@
     per = got.shape[1] // rows
     wide = peers * rows
     col = pl.multiple_of(lax.axis_index("mp") * width, LANES)
-    for o in range(owners):
-        line = got[o * peers, 0:rows, :].astype(F32)[passes : passes + 1]
-        info_v[o : o + 1, :] = line.astype(jnp.int32)
+    lines = [got[o * peers, 0:rows, :].astype(F32)[passes : passes + 1] for o in range(owners)]
+    lines += [jnp.zeros((1, LANES), F32)] * (info_v.shape[1] - owners)
+    info = jnp.concatenate(lines, axis=0).astype(jnp.int32)
+    row = info * DIGIT + pltpu.roll(info, LANES - capacity, 1)
+    row = jnp.clip(row, 0, lists_own - 1)
+    place = pltpu.roll(info, LANES - 2 * capacity, 1)
+    first = lax.div(row, SUB)
+    base = lax.broadcasted_iota(jnp.int32, info.shape, 0) * wide - 1
+    info_v[0] = first
+    info_v[1] = row - first * SUB
+    info_v[2] = jnp.where((place > 0) & (place <= wide), place + base, -1)
     info_copy = pltpu.make_async_copy(info_v, info_s, info_sem)
     info_copy.start()
     info_copy.wait()
     entries = [(o, k) for o in range(owners) for k in range(capacity)]
-
-    def row_copy(n, first):
-        return pltpu.make_async_copy(
-            cents.at[pl.ds(first, SUB), pl.ds(col, width)], rows_in.at[n], row_sems.at[n]
-        )
-
-    which = []
     for n, (o, k) in enumerate(entries):
-        row = jnp.clip(info_s[o, k] * DIGIT + info_s[o, capacity + k], 0, lists_own - 1)
-        first = lax.div(row, SUB) * SUB
-        row_copy(n, pl.multiple_of(first, SUB)).start()
-        which.append(row - first)
-    total = None
-    for q in range(per):
-        x = got[:, q * rows : (q + 1) * rows, :].reshape(owners * peers * rows, LANES)
-        y = jnp.dot(x, head[q * LANES : (q + 1) * LANES, :], preferred_element_type=F32)
-        total = y if total is None else total + y
+        pltpu.make_async_copy(
+            cents.at[pl.ds(pl.multiple_of(info_s[0, o, k] * SUB, SUB), SUB), pl.ds(col, width)],
+            rows_in.at[n],
+            row_sem,
+        ).start()
+    x = jnp.concatenate(
+        [
+            got[:, q * rows : (q + 1) * rows, :].reshape(owners * peers * rows, LANES)
+            for q in range(per)
+        ],
+        axis=1,
+    )
+    total = jnp.dot(x, head[...], preferred_element_type=F32)
     lane = lax.broadcasted_iota(jnp.int32, (1, LANES), 1)
+    spots = lax.broadcasted_iota(jnp.int32, (owners * wide, LANES), 0)
     share = LANES // SUB
-    for n in range(len(entries)):
-        row_copy(n, 0).wait()
+    chosen = []
     for start in range(0, len(entries), share):
-        part = entries[start : start + share]
         target = jnp.full((1, LANES), -1, jnp.int32)
-        for m, (o, k) in enumerate(part):
-            place = info_s[o, 2 * capacity + k]
-            at = jnp.where((place > 0) & (place <= wide), o * wide + place - 1, -1)
-            target = jnp.where(lane == m * SUB + which[start + m], at, target)
-        depth = len(part) * SUB
-        spots = lax.broadcasted_iota(jnp.int32, (owners * wide, LANES), 0)
-        chosen = jnp.where(spots == target, 1.0, 0.0).astype(BF16)[:, :depth]
-        lines = rows_in[start : start + len(part)].reshape(depth, width)
-        total = total - jnp.dot(chosen, lines, preferred_element_type=F32)
+        for m, (o, k) in enumerate(entries[start : start + share]):
+            target = jnp.where(lane == m * SUB + info_s[1, o, k], info_s[2, o, k], target)
+        chosen.append(jnp.where(spots == target, 1.0, 0.0).astype(BF16))
+    depth = len(entries) * SUB
+    chosen = jnp.concatenate(chosen, axis=1)[:, :depth]
+    pltpu.make_async_copy(rows_in, rows_in, row_sem).wait()
+    total = total - jnp.dot(
+        chosen, rows_in[...].reshape(depth, width), preferred_element_type=F32
+    )
     acc[...] = total.reshape(owners, wide, width)
     core = lax.axis_index("core")
     group = peers * passes
@@ -319,7 +328,7 @@
         out_specs=(vmem, vmem),
         scratch_shapes=[
             pltpu.VMEM((passes * steps, STEP, width), BF16),
-            pltpu.VMEM((2, STEP, LANES), F32),
+            pltpu.VMEM((2, STEP, 2 * LANES), BF16),
             pltpu.VMEM((passes, SUB, width), F32),
             pltpu.VMEM((padded, LANES), jnp.int32),
             pltpu.VMEM((width // LANES, LANES), BF16),
@@ -366,13 +375,13 @@
         in_specs=[vmem, vmem, hbm],
         out_specs=(vmem, vmem),
         scratch_shapes=[
-            pltpu.VMEM((lead, LANES), jnp.int32),
-            pltpu.SMEM((lead, LANES), jnp.int32),
+            pltpu.VMEM((3, lead, LANES), jnp.int32),
+            pltpu.SMEM((3, lead, LANES), jnp.int32),
             pltpu.VMEM((owners, peers * SUB, cols), F32),
             pltpu.VMEM((owners * capacity, SUB, cols), BF16),
             pltpu.VMEM((CORES, half, cols), F32),
             pltpu.SemaphoreType.DMA,
-            pltpu.SemaphoreType.DMA((owners * capacity,)),
+            pltpu.SemaphoreType.DMA,
         ],
         compiler_params=pltpu.CompilerParams(vmem_limit_bytes=8 * 2**20),
         name="project",

time: 41.5 us -> 41.1 us (level)
  starting transfers between devices: 1.02 us -> 0.37 us
  Pallas kernels: 8.34 us -> 8.83 us
    ppermute x1, starting transfers between devices: 1.02 us -> 0.37 us  [per_device(): lax.ppermute(other, 'core', [(c, (c + 1) % CORES) for c in range(CORES)])]
    pallas_call x1, Pallas kernels: 2.67 us -> 3.12 us  [per_device(): pl.pallas_call(functools.partial(project_kernel, owners=owners, peers=pee...]
where the time goes in v3:
time: 41.1 us; the launch traced here: 40.9 us
  blocking collectives  30.1 us (73%)
  Pallas kernels  8.83 us (21%)
  waiting for transfers between devices  0.93 us (2%)
  between operations  0.66 us (2%)
    all_to_all x1, blocking collectives, per_device(): got = lax.all_to_all(blocks, ('chip', 'core', 'mp'), 0, 0, tiled=True)  17.2 us
    all_to_all x1, blocking collectives, per_device(): parts = lax.all_to_all(parts, ('chip', 'mp'), 0, 0, tiled=True)  12.9 us
    pallas_call x1, Pallas kernels, pool_call(): pl.pallas_call(functools.partial(pool_kernel, owners=owners, peers=peers,...  4.75 us
    pallas_call x1, Pallas kernels, per_device(): pl.pallas_call(functools.partial(project_kernel, owners=owners, peers=pee...  3.12 us
    ppermute x1, waiting for transfers between devices, per_device(): lax.ppermute(other, 'core', [(c, (c + 1) % CORES) for c in range(CORES)])  0.93 us
  transfers between devices with their start and end apart: 1, of which 1 were waited for; matrix products, arithmetic and copies ran while one was open for 0% of the time, Pallas kernels for 0%

profile of v3, /device:TPU:0, one launch (start us, length us, event | category | flops | bytes accessed | tf_op | source)
XLA Modules:
  0.0 40.9 jit_solution(4706406350196293582)
XLA Ops:
  0.6 0.0 copy-start
  0.6 4.7 %pool.1 = (bf16[32,32,128]{2,1,0:T(8,128)(2,1)S(1)}, bf16[512,256]{1,0:T(8,128)(2,1)S(1)}) custom-call(s32[6]{0:T(128)} %lens_hbm.1, s32[24]{0:T(128)} %ids_hbm.1, bf16[6,256,4096]{2,1,0:T(8,128)(2,1)} %hidden.1, s32[512,128]{1,0:T(8,128)} %bitcast.3, bf16[32,128]{1,0:T(8,128)(2,1)} %bitcast.4, bf16[512,256]{1,0:T(8,128)(2,1)} %head.1), custom_call_target="tpu_custom_call" | custom-call | tf_op jit(solution)/shard_map/pool/pallas_call | solution.py:319
  5.4 17.2 %all_to_all.10.got = bf16[32,32,128]{2,1,0:T(8,128)(2,1)S(1)} all-to-all(bf16[32,32,128]{2,1,0:T(8,128)(2,1)S(1)} %get-tuple-element.8), channel_id=1, replica_groups=mesh['chip'=4,'core'=2,'mp'=4] {'chip','core','mp'}, dimensions={0} | all-to-all | bytes 524288 | tf_op jit(solution)/shard_map/all_to_all | solution.py:365
  22.6 3.1 %project.1 = (f32[96,256]{1,0:T(8,128)S(1)}, bf16[96,256]{1,0:T(8,128)(2,1)S(1)}) custom-call(bf16[32,32,128]{2,1,0:T(8,128)(2,1)S(1)} %all_to_all.10.got, bf16[512,256]{1,0:T(8,128)(2,1)S(1)} %get-tuple-element.9.head, bf16[8192,1024]{1,0:T(8,128)(2,1)} %cents.1), custom_call_target="tpu_custom_call" | custom-call | tf_op jit(solution)/shard_map/project/pallas_call | solution.py:367
  25.7 0.4 collective-permute-start
  26.1 0.9 %collective-permute-done.other = bf16[96,256]{1,0:T(8,128)(2,1)S(1)} collective-permute-done((bf16[96,256]{1,0:T(8,128)(2,1)S(1)}, bf16[96,256]{1,0:T(8,128)(2,1)S(1)}, u32[]{:S(2)}, u32[]{:S(2)}) %collective-permute-start) | collective-permute-done | bytes 49184 | tf_op jit(solution)/shard_map/ppermute | solution.py:389
  27.0 0.0 copy-done
  27.0 0.2 rotate.1
  27.3 12.9 %all_to_all.11.parts = bf16[16,24,256]{2,1,0:T(8,128)(2,1)S(1)} all-to-all(bf16[16,24,256]{2,1,0:T(8,128)(2,1)S(1)} %rotate.1), channel_id=1, replica_groups=mesh['chip'=4,'core'=2,'mp'=4] {'chip','mp'}, dimensions={0} | all-to-all | bytes 393216 | tf_op jit(solution)/shard_map/all_to_all | solution.py:398
  40.2 0.7 %quantize.1 = (bf16[24,256]{1,0:T(8,128)(2,1)}, bf16[4,24]{1,0:T(4,128)(2,1)}) custom-call(bf16[16,24,256]{2,1,0:T(8,128)(2,1)S(1)} %all_to_all.11.parts), custom_call_target="tpu_custom_call" | custom-call | tf_op jit(solution)/shard_map/quantize/pallas_call | solution.py:399
Async XLA Ops:
  0.6 26.4 %copy-start = (bf16[256,1024]{1,0:T(8,128)(2,1)S(1)}, bf16[256,1024]{1,0:T(8,128)(2,1)}, u32[]{:S(2)}) copy-start(bf16[256,1024]{1,0:T(8,128)(2,1)} %rotation.1) | copy-start | bytes 1572868
  25.7 1.3 %collective-permute-start = (bf16[96,256]{1,0:T(8,128)(2,1)S(1)}, bf16[96,256]{1,0:T(8,128)(2,1)S(1)}, u32[]{:S(2)}, u32[]{:S(2)}) collective-permute-start(bf16[96,256]{1,0:T(8,128)(2,1)S(1)} %get-tuple-element.11), channel_id=1, source_target_pairs={{0,4},{4,0},{1,5},{5,1},{2,6},{6,2},{3,7},{7,3},{8,12},{12,8},{9,1... | collective-permute-start | bytes 147464 | tf_op jit(solution)/shard_map/ppermute | solution.py:389

commit v4 on v3

--- a/solution.py
+++ b/solution.py
@@ -208,26 +208,39 @@
 
 
 def project_kernel(
-    got, head, cents, own, other, info_v, info_s, acc, rows_in, packed, info_sem, row_sem,
+    got, head, cents, own, other, info_v, info_s, rows_in, info_sem, row_sem,
     *, owners, peers, passes, capacity,
 ):
-    rows = SUB
     width = head.shape[1]
     lists_own = cents.shape[0]
-    per = got.shape[1] // rows
-    wide = peers * rows
+    per = got.shape[1] // SUB
+    wide = peers * SUB
+    group = peers * passes
+    half = owners // CORES * group
+    core = lax.axis_index("core")
     col = pl.multiple_of(lax.axis_index("mp") * width, LANES)
-    lines = [got[o * peers, 0:rows, :].astype(F32)[passes : passes + 1] for o in range(owners)]
+
+    def final_row(o, at):
+        peer = lax.div(at, SUB)
+        chip = lax.div(o, CORES)
+        away = jnp.where(o - chip * CORES == core, 0, half)
+        return away + chip * group + peer * passes + (at - peer * SUB)
+
+    lines = [got[o * peers, 0:SUB, :].astype(F32)[passes : passes + 1] for o in range(owners)]
     lines += [jnp.zeros((1, LANES), F32)] * (info_v.shape[1] - owners)
     info = jnp.concatenate(lines, axis=0).astype(jnp.int32)
     row = info * DIGIT + pltpu.roll(info, LANES - capacity, 1)
     row = jnp.clip(row, 0, lists_own - 1)
     place = pltpu.roll(info, LANES - 2 * capacity, 1)
     first = lax.div(row, SUB)
-    base = lax.broadcasted_iota(jnp.int32, info.shape, 0) * wide - 1
+    real = (place > 0) & (place <= wide)
     info_v[0] = first
     info_v[1] = row - first * SUB
-    info_v[2] = jnp.where((place > 0) & (place <= wide), place + base, -1)
+    info_v[2] = jnp.where(
+        real,
+        final_row(lax.broadcasted_iota(jnp.int32, info.shape, 0), jnp.where(real, place - 1, 0)),
+        -1,
+    )
     info_copy = pltpu.make_async_copy(info_v, info_s, info_sem)
     info_copy.start()
     info_copy.wait()
@@ -238,40 +251,40 @@
             rows_in.at[n],
             row_sem,
         ).start()
-    x = jnp.concatenate(
-        [
-            got[:, q * rows : (q + 1) * rows, :].reshape(owners * peers * rows, LANES)
-            for q in range(per)
-        ],
-        axis=1,
-    )
-    total = jnp.dot(x, head[...], preferred_element_type=F32)
     lane = lax.broadcasted_iota(jnp.int32, (1, LANES), 1)
-    spots = lax.broadcasted_iota(jnp.int32, (owners * wide, LANES), 0)
+    spots = lax.broadcasted_iota(jnp.int32, (CORES * half, LANES), 0)
     share = LANES // SUB
     chosen = []
     for start in range(0, len(entries), share):
         target = jnp.full((1, LANES), -1, jnp.int32)
         for m, (o, k) in enumerate(entries[start : start + share]):
             target = jnp.where(lane == m * SUB + info_s[1, o, k], info_s[2, o, k], target)
-        chosen.append(jnp.where(spots == target, 1.0, 0.0).astype(BF16))
+        chosen.append(jnp.where(spots == target, -1.0, 0.0).astype(BF16))
     depth = len(entries) * SUB
     chosen = jnp.concatenate(chosen, axis=1)[:, :depth]
+    sources = owners * wide
+    order = []
+    for start in range(0, sources, LANES):
+        at = lane + start
+        o = lax.div(at, wide)
+        at = at - o * wide
+        target = jnp.where(at - lax.div(at, SUB) * SUB < passes, final_row(o, at), -1)
+        order.append(jnp.where(spots == target, 1.0, 0.0).astype(BF16))
+    x = jnp.concatenate(
+        [
+            got[:, q * SUB : (q + 1) * SUB, :].reshape(sources, LANES)
+            for q in range(per)
+        ],
+        axis=1,
+    )
+    x = jnp.dot(jnp.concatenate(order, axis=1), x, preferred_element_type=F32).astype(BF16)
+    total = jnp.dot(x, head[...], preferred_element_type=F32)
     pltpu.make_async_copy(rows_in, rows_in, row_sem).wait()
-    total = total - jnp.dot(
+    total = total + jnp.dot(
         chosen, rows_in[...].reshape(depth, width), preferred_element_type=F32
     )
-    acc[...] = total.reshape(owners, wide, width)
-    core = lax.axis_index("core")
-    group = peers * passes
-    for side in range(CORES):
-        for c in range(owners // CORES):
-            x = acc[c * CORES + (core if side == 0 else 1 - core)]
-            for j in range(peers):
-                at = c * group + j * passes
-                packed[side, at : at + passes, :] = x[j * rows : j * rows + passes]
-    own[...] = packed[0]
-    other[...] = packed[1].astype(BF16)
+    own[...] = total[:half]
+    other[...] = total[half:].astype(BF16)
 
 
 def rotate_kernel(own, other, rotation, out, *, peers):
@@ -377,9 +390,7 @@
         scratch_shapes=[
             pltpu.VMEM((3, lead, LANES), jnp.int32),
             pltpu.SMEM((3, lead, LANES), jnp.int32),
-            pltpu.VMEM((owners, peers * SUB, cols), F32),
             pltpu.VMEM((owners * capacity, SUB, cols), BF16),
-            pltpu.VMEM((CORES, half, cols), F32),
             pltpu.SemaphoreType.DMA,
             pltpu.SemaphoreType.DMA,
         ],

time: 41.1 us -> 41.4 us (level)
  Pallas kernels: 8.83 us -> 8.06 us
  starting transfers between devices: 0.37 us -> 1.12 us
    pallas_call x1, Pallas kernels: 3.12 us -> 2.2 us  [per_device(): pl.pallas_call(functools.partial(project_kernel, owners=owners, peers=pee...]
    ppermute x1, starting transfers between devices: 0.37 us -> 1.12 us  [per_device(): lax.ppermute(other, 'core', [(c, (c + 1) % CORES) for c in range(CORES)])]
where the time goes in v4:
time: 41.4 us; the launch traced here: 41.1 us
  blocking collectives  30.3 us (73%)
  Pallas kernels  8.06 us (19%)
  starting transfers between devices  1.12 us (3%)
  waiting for transfers between devices  0.88 us (2%)
  between operations  0.66 us (2%)
    all_to_all x1, blocking collectives, per_device(): got = lax.all_to_all(blocks, ('chip', 'core', 'mp'), 0, 0, tiled=True)  17.2 us
    all_to_all x1, blocking collectives, per_device(): parts = lax.all_to_all(parts, ('chip', 'mp'), 0, 0, tiled=True)  13.1 us
    pallas_call x1, Pallas kernels, pool_call(): pl.pallas_call(functools.partial(pool_kernel, owners=owners, peers=peers,...  4.9 us
    pallas_call x1, Pallas kernels, per_device(): pl.pallas_call(functools.partial(project_kernel, owners=owners, peers=pee...  2.2 us
    ppermute x1, starting transfers between devices, per_device(): lax.ppermute(other, 'core', [(c, (c + 1) % CORES) for c in range(CORES)])  1.12 us
    ppermute x1, waiting for transfers between devices, per_device(): lax.ppermute(other, 'core', [(c, (c + 1) % CORES) for c in range(CORES)])  0.88 us
  transfers between devices with their start and end apart: 1, of which 1 were waited for; matrix products, arithmetic and copies ran while one was open for 0% of the time, Pallas kernels for 0%

profile of v4, /device:TPU:0, one launch (start us, length us, event | category | flops | bytes accessed | tf_op | source)
XLA Modules:
  0.0 41.1 jit_solution(9907398779566196978)
XLA Ops:
  0.6 0.0 copy-start
  0.6 4.9 %pool.1 = (bf16[32,32,128]{2,1,0:T(8,128)(2,1)S(1)}, bf16[512,256]{1,0:T(8,128)(2,1)S(1)}) custom-call(s32[6]{0:T(128)} %lens_hbm.1, s32[24]{0:T(128)} %ids_hbm.1, bf16[6,256,4096]{2,1,0:T(8,128)(2,1)} %hidden.1, s32[512,128]{1,0:T(8,128)} %bitcast.3, bf16[32,128]{1,0:T(8,128)(2,1)} %bitcast.4, bf16[512,256]{1,0:T(8,128)(2,1)} %head.1), custom_call_target="tpu_custom_call" | custom-call | tf_op jit(solution)/shard_map/pool/pallas_call | solution.py:332
  5.6 17.2 %all_to_all.10.got = bf16[32,32,128]{2,1,0:T(8,128)(2,1)S(1)} all-to-all(bf16[32,32,128]{2,1,0:T(8,128)(2,1)S(1)} %get-tuple-element.8), channel_id=1, replica_groups=mesh['chip'=4,'core'=2,'mp'=4] {'chip','core','mp'}, dimensions={0} | all-to-all | bytes 524288 | tf_op jit(solution)/shard_map/all_to_all | solution.py:378
  22.8 2.2 %project.1 = (f32[96,256]{1,0:T(8,128)S(1)}, bf16[96,256]{1,0:T(8,128)(2,1)S(1)}) custom-call(bf16[32,32,128]{2,1,0:T(8,128)(2,1)S(1)} %all_to_all.10.got, bf16[512,256]{1,0:T(8,128)(2,1)S(1)} %get-tuple-element.9.head, bf16[8192,1024]{1,0:T(8,128)(2,1)} %cents.1), custom_call_target="tpu_custom_call" | custom-call | tf_op jit(solution)/shard_map/project/pallas_call | solution.py:380
  25.0 1.1 %collective-permute-start = (bf16[96,256]{1,0:T(8,128)(2,1)S(1)}, bf16[96,256]{1,0:T(8,128)(2,1)S(1)}, u32[]{:S(2)}, u32[]{:S(2)}) collective-permute-start(bf16[96,256]{1,0:T(8,128)(2,1)S(1)} %get-tuple-element.11), channel_id=1, source_target_pairs={{0,4},{4,0},{1,5},{5,1},{2,6},{6,2},{3,7},{7,3},{8,12},{12,8},{9,1... | collective-permute-start | bytes 147464 | tf_op jit(solution)/shard_map/ppermute | solution.py:400
  26.1 0.9 %collective-permute-done.other = bf16[96,256]{1,0:T(8,128)(2,1)S(1)} collective-permute-done((bf16[96,256]{1,0:T(8,128)(2,1)S(1)}, bf16[96,256]{1,0:T(8,128)(2,1)S(1)}, u32[]{:S(2)}, u32[]{:S(2)}) %collective-permute-start) | collective-permute-done | bytes 49184 | tf_op jit(solution)/shard_map/ppermute | solution.py:400
  27.0 0.0 copy-done
  27.0 0.2 rotate.1
  27.2 13.1 %all_to_all.11.parts = bf16[16,24,256]{2,1,0:T(8,128)(2,1)S(1)} all-to-all(bf16[16,24,256]{2,1,0:T(8,128)(2,1)S(1)} %rotate.1), channel_id=1, replica_groups=mesh['chip'=4,'core'=2,'mp'=4] {'chip','mp'}, dimensions={0} | all-to-all | bytes 393216 | tf_op jit(solution)/shard_map/all_to_all | solution.py:409
  40.3 0.7 %quantize.1 = (bf16[24,256]{1,0:T(8,128)(2,1)}, bf16[4,24]{1,0:T(4,128)(2,1)}) custom-call(bf16[16,24,256]{2,1,0:T(8,128)(2,1)S(1)} %all_to_all.11.parts), custom_call_target="tpu_custom_call" | custom-call | tf_op jit(solution)/shard_map/quantize/pallas_call | solution.py:410
Async XLA Ops:
  0.6 26.3 %copy-start = (bf16[256,1024]{1,0:T(8,128)(2,1)S(1)}, bf16[256,1024]{1,0:T(8,128)(2,1)}, u32[]{:S(2)}) copy-start(bf16[256,1024]{1,0:T(8,128)(2,1)} %rotation.1) | copy-start | bytes 1572868
  25.0 2.0 %collective-permute-start = (bf16[96,256]{1,0:T(8,128)(2,1)S(1)}, bf16[96,256]{1,0:T(8,128)(2,1)S(1)}, u32[]{:S(2)}, u32[]{:S(2)}) collective-permute-start(bf16[96,256]{1,0:T(8,128)(2,1)S(1)} %get-tuple-element.11), channel_id=1, source_target_pairs={{0,4},{4,0},{1,5},{5,1},{2,6},{6,2},{3,7},{7,3},{8,12},{12,8},{9,1... | collective-permute-start | bytes 147464 | tf_op jit(solution)/shard_map/ppermute | solution.py:400

commit v5 on v4

--- a/solution.py
+++ b/solution.py
@@ -36,7 +36,7 @@
     steps = length // STEP
     tiles = width // LANES
     per = tiles // owners
-    rows = out.shape[1] // per
+    pairs = -(-passes // 2)
 
     def chunk_copy(p, c):
         return pltpu.make_async_copy(
@@ -163,7 +163,7 @@
     peer = jnp.zeros(shape, jnp.int32)
     for j in range(1, peers):
         peer = peer + (line >= j * passes).astype(jnp.int32)
-    place = line + peer * (rows - passes) + 1
+    place = line + peer * (SUB - passes) + 1
     entry = jnp.where(lane == rank, high, 0)
     entry = jnp.where(lane == rank + capacity, low, entry)
     entry = jnp.where(lane == rank + 2 * capacity, place, entry)
@@ -200,11 +200,14 @@
                 parts = merged
                 bit //= 2
             tile = parts[0] * gain[t : t + 1].astype(F32) * inverse
-            if q == 0:
-                tile = jnp.where(sub == passes, jnp.broadcast_to(info, (SUB, LANES)), tile)
-            tile = tile.astype(BF16)
-            for j in range(peers):
-                out[o * peers + j, q * rows : (q + 1) * rows, :] = tile
+            for n in range(pairs):
+                piece = tile[2 * n : 2 * n + 2].astype(BF16)
+                at = (q * pairs + n) * LANES
+                for j in range(peers):
+                    out[o * peers + j, :, at : at + LANES] = piece
+        info = jnp.broadcast_to(info, (2, LANES)).astype(BF16)
+        for j in range(peers):
+            out[o * peers + j, :, per * pairs * LANES :] = info
 
 
 def project_kernel(
@@ -213,7 +216,8 @@
 ):
     width = head.shape[1]
     lists_own = cents.shape[0]
-    per = got.shape[1] // SUB
+    pairs = -(-passes // 2)
+    per = (got.shape[2] // LANES - 1) // pairs
     wide = peers * SUB
     group = peers * passes
     half = owners // CORES * group
@@ -226,7 +230,8 @@
         away = jnp.where(o - chip * CORES == core, 0, half)
         return away + chip * group + peer * passes + (at - peer * SUB)
 
-    lines = [got[o * peers, 0:SUB, :].astype(F32)[passes : passes + 1] for o in range(owners)]
+    tail = per * pairs * LANES
+    lines = [got[o * peers, :, tail:].astype(F32)[0:1] for o in range(owners)]
     lines += [jnp.zeros((1, LANES), F32)] * (info_v.shape[1] - owners)
     info = jnp.concatenate(lines, axis=0).astype(jnp.int32)
     row = info * DIGIT + pltpu.roll(info, LANES - capacity, 1)
@@ -262,22 +267,35 @@
         chosen.append(jnp.where(spots == target, -1.0, 0.0).astype(BF16))
     depth = len(entries) * SUB
     chosen = jnp.concatenate(chosen, axis=1)[:, :depth]
-    sources = owners * wide
+    sources = owners * peers
+    depth_in = pairs * sources * 2
     order = []
-    for start in range(0, sources, LANES):
+    for start in range(0, depth_in, LANES):
         at = lane + start
-        o = lax.div(at, wide)
-        at = at - o * wide
-        target = jnp.where(at - lax.div(at, SUB) * SUB < passes, final_row(o, at), -1)
+        pair = lax.div(at, sources * 2)
+        at = at - pair * sources * 2
+        source = lax.div(at, 2)
+        p = pair * 2 + at - source * 2
+        o = lax.div(source, peers)
+        target = jnp.where(p < passes, final_row(o, (source - o * peers) * SUB + p), -1)
         order.append(jnp.where(spots == target, 1.0, 0.0).astype(BF16))
+    order = jnp.concatenate(order, axis=1)[:, :depth_in]
     x = jnp.concatenate(
         [
-            got[:, q * SUB : (q + 1) * SUB, :].reshape(sources, LANES)
-            for q in range(per)
+            jnp.concatenate(
+                [
+                    got[:, :, (q * pairs + n) * LANES : (q * pairs + n + 1) * LANES].reshape(
+                        sources * 2, LANES
+                    )
+                    for q in range(per)
+                ],
+                axis=1,
+            )
+            for n in range(pairs)
         ],
-        axis=1,
-    )
-    x = jnp.dot(jnp.concatenate(order, axis=1), x, preferred_element_type=F32).astype(BF16)
+        axis=0,
+    )
+    x = jnp.dot(order, x, preferred_element_type=F32).astype(BF16)
     total = jnp.dot(x, head[...], preferred_element_type=F32)
     pltpu.make_async_copy(rows_in, rows_in, row_sem).wait()
     total = total + jnp.dot(
@@ -334,7 +352,7 @@
             pool_kernel, owners=owners, peers=peers, lists_own=lists_own, capacity=capacity
         ),
         out_shape=(
-            pltpu.VMEM((owners * peers, per * SUB, LANES), BF16),
+            pltpu.VMEM((owners * peers, 2, (per * -(-passes // 2) + 1) * LANES), BF16),
             pltpu.VMEM(head.shape, BF16),
         ),
         in_specs=[hbm] * 6,

time: 41.4 us -> 40.1 us (0.969)
  blocking collectives: 30.3 us -> 29.1 us
  starting transfers between devices: 1.12 us -> 0.07 us
  Pallas kernels: 8.06 us -> 8.71 us
    ppermute x1, starting transfers between devices: 1.12 us -> 0.07 us  [per_device(): lax.ppermute(other, 'core', [(c, (c + 1) % CORES) for c in range(CORES)])]
    pallas_call x1, Pallas kernels: 2.2 us -> 3.12 us  [per_device(): pl.pallas_call(functools.partial(project_kernel, owners=owners, peers=pee...]
    all_to_all x1, blocking collectives: 13.1 us -> 12.5 us  [per_device(): parts = lax.all_to_all(parts, ('chip', 'mp'), 0, 0, tiled=True)]
    all_to_all x1, blocking collectives: 17.2 us -> 16.7 us  [per_device(): got = lax.all_to_all(blocks, ('chip', 'core', 'mp'), 0, 0, tiled=True)]
where the time goes in v5:
time: 40.1 us; the launch traced here: 39.8 us
  blocking collectives  29.1 us (73%)
  Pallas kernels  8.71 us (22%)
  waiting for transfers between devices  1.22 us (3%)
  between operations  0.67 us (2%)
    all_to_all x1, blocking collectives, per_device(): got = lax.all_to_all(blocks, ('chip', 'core', 'mp'), 0, 0, tiled=True)  16.7 us
    all_to_all x1, blocking collectives, per_device(): parts = lax.all_to_all(parts, ('chip', 'mp'), 0, 0, tiled=True)  12.5 us
    pallas_call x1, Pallas kernels, pool_call(): pl.pallas_call(functools.partial(pool_kernel, owners=owners, peers=peers,...  4.62 us
    pallas_call x1, Pallas kernels, per_device(): pl.pallas_call(functools.partial(project_kernel, owners=owners, peers=pee...  3.12 us
    ppermute x1, waiting for transfers between devices, per_device(): lax.ppermute(other, 'core', [(c, (c + 1) % CORES) for c in range(CORES)])  1.22 us
  transfers between devices with their start and end apart: 1, of which 1 were waited for; matrix products, arithmetic and copies ran while one was open for 0% of the time, Pallas kernels for 0%

profile of v5, /device:TPU:0, one launch (start us, length us, event | category | flops | bytes accessed | tf_op | source)
XLA Modules:
  0.0 39.8 jit_solution(6167210740767590411)
XLA Ops:
  0.6 0.0 copy-start
  0.6 4.6 %pool.1 = (bf16[32,2,1664]{2,1,0:T(2,128)(2,1)S(1)}, bf16[512,256]{1,0:T(8,128)(2,1)S(1)}) custom-call(s32[6]{0:T(128)} %lens_hbm.1, s32[24]{0:T(128)} %ids_hbm.1, bf16[6,256,4096]{2,1,0:T(8,128)(2,1)} %hidden.1, s32[512,128]{1,0:T(8,128)} %bitcast.3, bf16[32,128]{1,0:T(8,128)(2,1)} %bitcast.4, bf16[512,256]{1,0:T(8,128)(2,1)} %head.1), custom_call_target="tpu_custom_call" | custom-call | tf_op jit(solution)/shard_map/pool/pallas_call | solution.py:350
  5.3 16.7 %all_to_all.10.got = bf16[32,2,1664]{2,1,0:T(2,128)(2,1)S(1)} all-to-all(bf16[32,2,1664]{2,1,0:T(2,128)(2,1)S(1)} %get-tuple-element.8), channel_id=1, replica_groups=mesh['chip'=4,'core'=2,'mp'=4] {'chip','core','mp'}, dimensions={0} | all-to-all | bytes 425984 | tf_op jit(solution)/shard_map/all_to_all | solution.py:396
  21.9 3.1 %project.1 = (f32[96,256]{1,0:T(8,128)S(1)}, bf16[96,256]{1,0:T(8,128)(2,1)S(1)}) custom-call(bf16[32,2,1664]{2,1,0:T(2,128)(2,1)S(1)} %all_to_all.10.got, bf16[512,256]{1,0:T(8,128)(2,1)S(1)} %get-tuple-element.9.head, bf16[8192,1024]{1,0:T(8,128)(2,1)} %cents.1), custom_call_target="tpu_custom_call" | custom-call | tf_op jit(solution)/shard_map/project/pallas_call | solution.py:398
  25.1 0.1 collective-permute-start
  25.1 1.2 %collective-permute-done.other = bf16[96,256]{1,0:T(8,128)(2,1)S(1)} collective-permute-done((bf16[96,256]{1,0:T(8,128)(2,1)S(1)}, bf16[96,256]{1,0:T(8,128)(2,1)S(1)}, u32[]{:S(2)}, u32[]{:S(2)}) %collective-permute-start) | collective-permute-done | bytes 49184 | tf_op jit(solution)/shard_map/ppermute | solution.py:418
  26.4 0.0 copy-done
  26.4 0.2 rotate.1
  26.6 12.5 %all_to_all.11.parts = bf16[16,24,256]{2,1,0:T(8,128)(2,1)S(1)} all-to-all(bf16[16,24,256]{2,1,0:T(8,128)(2,1)S(1)} %rotate.1), channel_id=1, replica_groups=mesh['chip'=4,'core'=2,'mp'=4] {'chip','mp'}, dimensions={0} | all-to-all | bytes 393216 | tf_op jit(solution)/shard_map/all_to_all | solution.py:427
  39.1 0.7 %quantize.1 = (bf16[24,256]{1,0:T(8,128)(2,1)}, bf16[4,24]{1,0:T(4,128)(2,1)}) custom-call(bf16[16,24,256]{2,1,0:T(8,128)(2,1)S(1)} %all_to_all.11.parts), custom_call_target="tpu_custom_call" | custom-call | tf_op jit(solution)/shard_map/quantize/pallas_call | solution.py:428
Async XLA Ops:
  0.6 25.7 %copy-start = (bf16[256,1024]{1,0:T(8,128)(2,1)S(1)}, bf16[256,1024]{1,0:T(8,128)(2,1)}, u32[]{:S(2)}) copy-start(bf16[256,1024]{1,0:T(8,128)(2,1)} %rotation.1) | copy-start | bytes 1572868
  25.1 1.3 %collective-permute-start = (bf16[96,256]{1,0:T(8,128)(2,1)S(1)}, bf16[96,256]{1,0:T(8,128)(2,1)S(1)}, u32[]{:S(2)}, u32[]{:S(2)}) collective-permute-start(bf16[96,256]{1,0:T(8,128)(2,1)S(1)} %get-tuple-element.11), channel_id=1, source_target_pairs={{0,4},{4,0},{1,5},{5,1},{2,6},{6,2},{3,7},{7,3},{8,12},{12,8},{9,1... | collective-permute-start | bytes 147464 | tf_op jit(solution)/shard_map/ppermute | solution.py:418

commit v6 on v5

--- a/solution.py
+++ b/solution.py
@@ -248,14 +248,14 @@
     )
     info_copy = pltpu.make_async_copy(info_v, info_s, info_sem)
     info_copy.start()
-    info_copy.wait()
     entries = [(o, k) for o in range(owners) for k in range(capacity)]
     for n, (o, k) in enumerate(entries):
         pltpu.make_async_copy(
-            cents.at[pl.ds(pl.multiple_of(info_s[0, o, k] * SUB, SUB), SUB), pl.ds(col, width)],
+            cents.at[pl.ds(pl.multiple_of(first[o, k] * SUB, SUB), SUB), pl.ds(col, width)],
             rows_in.at[n],
             row_sem,
         ).start()
+    info_copy.wait()
     lane = lax.broadcasted_iota(jnp.int32, (1, LANES), 1)
     spots = lax.broadcasted_iota(jnp.int32, (CORES * half, LANES), 0)
     share = LANES // SUB

time: 40.1 us -> 39.8 us (level); the launches traced: 39.8 us -> 39 us
  Pallas kernels: 8.71 us -> 7.54 us
    pallas_call x1, Pallas kernels: 3.12 us -> 2.11 us  [per_device(): pl.pallas_call(functools.partial(project_kernel, owners=owners, peers=pee...]
where the time goes in v6:
time: 39.8 us; the launch traced here: 39 us
  blocking collectives  29.5 us (74%)
  Pallas kernels  7.54 us (19%)
  waiting for transfers between devices  1.16 us (3%)
  between operations  0.66 us (2%)
    all_to_all x1, blocking collectives, per_device(): got = lax.all_to_all(blocks, ('chip', 'core', 'mp'), 0, 0, tiled=True)  16.7 us
    all_to_all x1, blocking collectives, per_device(): parts = lax.all_to_all(parts, ('chip', 'mp'), 0, 0, tiled=True)  12.8 us
    pallas_call x1, Pallas kernels, pool_call(): pl.pallas_call(functools.partial(pool_kernel, owners=owners, peers=peers,...  4.47 us
    pallas_call x1, Pallas kernels, per_device(): pl.pallas_call(functools.partial(project_kernel, owners=owners, peers=pee...  2.11 us
    ppermute x1, waiting for transfers between devices, per_device(): lax.ppermute(other, 'core', [(c, (c + 1) % CORES) for c in range(CORES)])  1.16 us
  transfers between devices with their start and end apart: 1, of which 1 were waited for; matrix products, arithmetic and copies ran while one was open for 0% of the time, Pallas kernels for 0%

profile of v6, /device:TPU:0, one launch (start us, length us, event | category | flops | bytes accessed | tf_op | source)
XLA Modules:
  0.0 39.0 jit_solution(15710181906227146715)
XLA Ops:
  0.6 0.0 copy-start
  0.6 4.5 %pool.1 = (bf16[32,2,1664]{2,1,0:T(2,128)(2,1)S(1)}, bf16[512,256]{1,0:T(8,128)(2,1)S(1)}) custom-call(s32[6]{0:T(128)} %lens_hbm.1, s32[24]{0:T(128)} %ids_hbm.1, bf16[6,256,4096]{2,1,0:T(8,128)(2,1)} %hidden.1, s32[512,128]{1,0:T(8,128)} %bitcast.3, bf16[32,128]{1,0:T(8,128)(2,1)} %bitcast.4, bf16[512,256]{1,0:T(8,128)(2,1)} %head.1), custom_call_target="tpu_custom_call" | custom-call | tf_op jit(solution)/shard_map/pool/pallas_call | solution.py:350
  5.1 16.7 %all_to_all.10.got = bf16[32,2,1664]{2,1,0:T(2,128)(2,1)S(1)} all-to-all(bf16[32,2,1664]{2,1,0:T(2,128)(2,1)S(1)} %get-tuple-element.8), channel_id=1, replica_groups=mesh['chip'=4,'core'=2,'mp'=4] {'chip','core','mp'}, dimensions={0} | all-to-all | bytes 425984 | tf_op jit(solution)/shard_map/all_to_all | solution.py:396
  21.8 2.1 %project.1 = (f32[96,256]{1,0:T(8,128)S(1)}, bf16[96,256]{1,0:T(8,128)(2,1)S(1)}) custom-call(bf16[32,2,1664]{2,1,0:T(2,128)(2,1)S(1)} %all_to_all.10.got, bf16[512,256]{1,0:T(8,128)(2,1)S(1)} %get-tuple-element.9.head, bf16[8192,1024]{1,0:T(8,128)(2,1)} %cents.1), custom_call_target="tpu_custom_call" | custom-call | tf_op jit(solution)/shard_map/project/pallas_call | solution.py:398
  23.9 0.1 collective-permute-start
  24.0 1.2 %collective-permute-done.other = bf16[96,256]{1,0:T(8,128)(2,1)S(1)} collective-permute-done((bf16[96,256]{1,0:T(8,128)(2,1)S(1)}, bf16[96,256]{1,0:T(8,128)(2,1)S(1)}, u32[]{:S(2)}, u32[]{:S(2)}) %collective-permute-start) | collective-permute-done | bytes 49184 | tf_op jit(solution)/shard_map/ppermute | solution.py:418
  25.2 0.0 copy-done
  25.2 0.2 rotate.1
  25.4 12.8 %all_to_all.11.parts = bf16[16,24,256]{2,1,0:T(8,128)(2,1)S(1)} all-to-all(bf16[16,24,256]{2,1,0:T(8,128)(2,1)S(1)} %rotate.1), channel_id=1, replica_groups=mesh['chip'=4,'core'=2,'mp'=4] {'chip','mp'}, dimensions={0} | all-to-all | bytes 393216 | tf_op jit(solution)/shard_map/all_to_all | solution.py:427
  38.3 0.7 %quantize.1 = (bf16[24,256]{1,0:T(8,128)(2,1)}, bf16[4,24]{1,0:T(4,128)(2,1)}) custom-call(bf16[16,24,256]{2,1,0:T(8,128)(2,1)S(1)} %all_to_all.11.parts), custom_call_target="tpu_custom_call" | custom-call | tf_op jit(solution)/shard_map/quantize/pallas_call | solution.py:428
Async XLA Ops:
  0.6 24.6 %copy-start = (bf16[256,1024]{1,0:T(8,128)(2,1)S(1)}, bf16[256,1024]{1,0:T(8,128)(2,1)}, u32[]{:S(2)}) copy-start(bf16[256,1024]{1,0:T(8,128)(2,1)} %rotation.1) | copy-start | bytes 1572868
  23.9 1.3 %collective-permute-start = (bf16[96,256]{1,0:T(8,128)(2,1)S(1)}, bf16[96,256]{1,0:T(8,128)(2,1)S(1)}, u32[]{:S(2)}, u32[]{:S(2)}) collective-permute-start(bf16[96,256]{1,0:T(8,128)(2,1)S(1)} %get-tuple-element.11), channel_id=1, source_target_pairs={{0,4},{4,0},{1,5},{5,1},{2,6},{6,2},{3,7},{7,3},{8,12},{12,8},{9,1... | collective-permute-start | bytes 147464 | tf_op jit(solution)/shard_map/ppermute | solution.py:418

commit v7 on v6

--- a/solution.py
+++ b/solution.py
@@ -211,7 +211,8 @@
 
 
 def project_kernel(
-    got, head, cents, own, other, info_v, info_s, rows_in, info_sem, row_sem,
+    got, head, cents, rotation, own, other, rotation_out, info_v, info_s, rows_in, info_sem, row_sem,
+    turn_sem,
     *, owners, peers, passes, capacity,
 ):
     width = head.shape[1]
@@ -255,6 +256,8 @@
             rows_in.at[n],
             row_sem,
         ).start()
+    turn_copy = pltpu.make_async_copy(rotation, rotation_out, turn_sem)
+    turn_copy.start()
     info_copy.wait()
     lane = lax.broadcasted_iota(jnp.int32, (1, LANES), 1)
     spots = lax.broadcasted_iota(jnp.int32, (CORES * half, LANES), 0)
@@ -303,6 +306,7 @@
     )
     own[...] = total[:half]
     other[...] = total[half:].astype(BF16)
+    turn_copy.wait()
 
 
 def rotate_kernel(own, other, rotation, out, *, peers):
@@ -395,26 +399,28 @@
     )
     got = lax.all_to_all(blocks, ("chip", "core", "mp"), 0, 0, tiled=True)
     half = owners // CORES * group
-    own, other = pl.pallas_call(
+    own, other, rotation = pl.pallas_call(
         functools.partial(
             project_kernel, owners=owners, peers=peers, passes=passes, capacity=capacity
         ),
         out_shape=(
             pltpu.VMEM((half, cols), F32),
             pltpu.VMEM((half, cols), BF16),
+            pltpu.VMEM(rotation.shape, BF16),
         ),
-        in_specs=[vmem, vmem, hbm],
-        out_specs=(vmem, vmem),
+        in_specs=[vmem, vmem, hbm, hbm],
+        out_specs=(vmem, vmem, vmem),
         scratch_shapes=[
             pltpu.VMEM((3, lead, LANES), jnp.int32),
             pltpu.SMEM((3, lead, LANES), jnp.int32),
             pltpu.VMEM((owners * capacity, SUB, cols), BF16),
             pltpu.SemaphoreType.DMA,
             pltpu.SemaphoreType.DMA,
+            pltpu.SemaphoreType.DMA,
         ],
         compiler_params=pltpu.CompilerParams(vmem_limit_bytes=8 * 2**20),
         name="project",
-    )(near(got), near(head), far(centroids))
+    )(near(got), near(head), far(centroids), far(rotation))
     other = lax.ppermute(other, "core", [(c, (c + 1) % CORES) for c in range(CORES)])
     parts = pl.pallas_call(
         functools.partial(rotate_kernel, peers=peers),

time: 39.8 us -> 39.6 us (level); the launches traced: 39 us -> 39.9 us
  blocking collectives: 29.5 us -> 30.4 us
    all_to_all x1, blocking collectives: 16.7 us -> 17.6 us  [per_device(): got = lax.all_to_all(blocks, ('chip', 'core', 'mp'), 0, 0, tiled=True)]
where the time goes in v7:
time: 39.6 us; the launch traced here: 39.9 us
  blocking collectives  30.4 us (77%)
  Pallas kernels  7.6 us (19%)
  waiting for transfers between devices  1.22 us (3%)
  between operations  0.66 us (2%)
    all_to_all x1, blocking collectives, per_device(): got = lax.all_to_all(blocks, ('chip', 'core', 'mp'), 0, 0, tiled=True)  17.6 us
    all_to_all x1, blocking collectives, per_device(): parts = lax.all_to_all(parts, ('chip', 'mp'), 0, 0, tiled=True)  12.8 us
    pallas_call x1, Pallas kernels, pool_call(): pl.pallas_call(functools.partial(pool_kernel, owners=owners, peers=peers,...  4.42 us
    pallas_call x1, Pallas kernels, per_device(): pl.pallas_call(functools.partial(project_kernel, owners=owners, peers=pee...  2.23 us
    ppermute x1, waiting for transfers between devices, per_device(): lax.ppermute(other, 'core', [(c, (c + 1) % CORES) for c in range(CORES)])  1.22 us
  transfers between devices with their start and end apart: 1, of which 1 were waited for; matrix products, arithmetic and copies ran while one was open for 0% of the time, Pallas kernels for 0%

profile of v7, /device:TPU:0, one launch (start us, length us, event | category | flops | bytes accessed | tf_op | source)
XLA Modules:
  0.0 39.9 jit_solution(8609721728698566034)
XLA Ops:
  0.6 4.4 %pool.1 = (bf16[32,2,1664]{2,1,0:T(2,128)(2,1)S(1)}, bf16[512,256]{1,0:T(8,128)(2,1)S(1)}) custom-call(s32[6]{0:T(128)} %lens_hbm.1, s32[24]{0:T(128)} %ids_hbm.1, bf16[6,256,4096]{2,1,0:T(8,128)(2,1)} %hidden.1, s32[512,128]{1,0:T(8,128)} %bitcast.3, bf16[32,128]{1,0:T(8,128)(2,1)} %bitcast.4, bf16[512,256]{1,0:T(8,128)(2,1)} %head.1), custom_call_target="tpu_custom_call" | custom-call | tf_op jit(solution)/shard_map/pool/pallas_call | solution.py:354
  5.1 17.6 %all_to_all.10.got = bf16[32,2,1664]{2,1,0:T(2,128)(2,1)S(1)} all-to-all(bf16[32,2,1664]{2,1,0:T(2,128)(2,1)S(1)} %get-tuple-element.9), channel_id=1, replica_groups=mesh['chip'=4,'core'=2,'mp'=4] {'chip','core','mp'}, dimensions={0} | all-to-all | bytes 425984 | tf_op jit(solution)/shard_map/all_to_all | solution.py:400
  22.7 2.2 %project.1 = (f32[96,256]{1,0:T(8,128)S(1)}, bf16[96,256]{1,0:T(8,128)(2,1)S(1)}, bf16[256,1024]{1,0:T(8,128)(2,1)S(1)}) custom-call(bf16[32,2,1664]{2,1,0:T(2,128)(2,1)S(1)} %all_to_all.10.got, bf16[512,256]{1,0:T(8,128)(2,1)S(1)} %get-tuple-element.10.head, bf16[8192,1024]{1,0:T(8,128)(2,1)} %cents.1, bf16[256,1024]{1,0:T(8,128)(2,1)} %rotation.1), custom_call_target="tpu_custom_call" | custom-call | tf_op jit(solution)/shard_map/project/pallas_call | solution.py:402
  24.9 0.1 collective-permute-start
  25.0 1.2 %collective-permute-done.other = bf16[96,256]{1,0:T(8,128)(2,1)S(1)} collective-permute-done((bf16[96,256]{1,0:T(8,128)(2,1)S(1)}, bf16[96,256]{1,0:T(8,128)(2,1)S(1)}, u32[]{:S(2)}, u32[]{:S(2)}) %collective-permute-start) | collective-permute-done | bytes 49184 | tf_op jit(solution)/shard_map/ppermute | solution.py:424
  26.2 0.2 rotate.1
  26.4 12.8 %all_to_all.11.parts = bf16[16,24,256]{2,1,0:T(8,128)(2,1)S(1)} all-to-all(bf16[16,24,256]{2,1,0:T(8,128)(2,1)S(1)} %rotate.1), channel_id=1, replica_groups=mesh['chip'=4,'core'=2,'mp'=4] {'chip','mp'}, dimensions={0} | all-to-all | bytes 393216 | tf_op jit(solution)/shard_map/all_to_all | solution.py:433
  39.2 0.7 %quantize.1 = (bf16[24,256]{1,0:T(8,128)(2,1)}, bf16[4,24]{1,0:T(4,128)(2,1)}) custom-call(bf16[16,24,256]{2,1,0:T(8,128)(2,1)S(1)} %all_to_all.11.parts), custom_call_target="tpu_custom_call" | custom-call | tf_op jit(solution)/shard_map/quantize/pallas_call | solution.py:434
Async XLA Ops:
  24.9 1.3 %collective-permute-start = (bf16[96,256]{1,0:T(8,128)(2,1)S(1)}, bf16[96,256]{1,0:T(8,128)(2,1)S(1)}, u32[]{:S(2)}, u32[]{:S(2)}) collective-permute-start(bf16[96,256]{1,0:T(8,128)(2,1)S(1)} %get-tuple-element.12), channel_id=1, source_target_pairs={{0,4},{4,0},{1,5},{5,1},{2,6},{6,2},{3,7},{7,3},{8,12},{12,8},{9,1... | collective-permute-start | bytes 147464 | tf_op jit(solution)/shard_map/ppermute | solution.py:424

commit v8 on v7

--- a/solution.py
+++ b/solution.py
@@ -321,7 +321,7 @@
             out[c * peers + j] = y[c * group : (c + 1) * group]
 
 
-def quantize_kernel(parts, codes, scales):
+def quantize_kernel(parts, codes_hbm, scales_hbm, codes, scales, sems):
     total = parts[0].astype(F32)
     for s in range(1, parts.shape[0]):
         total = total + parts[s].astype(F32)
@@ -338,7 +338,15 @@
             spread = jnp.where(inside, top, spread)
             table = jnp.where(lane == t * (LANES // BLOCK) + b, top, table)
         codes[:, t * LANES : (t + 1) * LANES] = (x / spread).astype(BF16)
+    copies = [
+        pltpu.make_async_copy(codes, codes_hbm, sems.at[0]),
+        pltpu.make_async_copy(scales, scales_hbm, sems.at[1]),
+    ]
+    copies[0].start()
     scales[...] = table.T[: scales.shape[0]].astype(BF16)
+    copies[1].start()
+    for copy in copies:
+        copy.wait()
 
 
 def pool_call(lengths, list_ids, hidden, list_slot, gain, head, *, owners, peers, lists_own):
@@ -438,7 +446,12 @@
             jax.ShapeDtypeStruct((cols // BLOCK, group), BF16),
         ),
         in_specs=[vmem],
-        out_specs=(vmem, vmem),
+        out_specs=(hbm, hbm),
+        scratch_shapes=[
+            pltpu.VMEM((group, cols), BF16),
+            pltpu.VMEM((cols // BLOCK, group), BF16),
+            pltpu.SemaphoreType.DMA((2,)),
+        ],
         compiler_params=pltpu.CompilerParams(vmem_limit_bytes=8 * 2**20),
         name="quantize",
     )(near(parts))

time: 39.6 us -> 40 us (1.010); the launches traced: 39.9 us -> 39.8 us
  no operation moved by 1% of the time
where the time goes in v8:
time: 40 us; the launch traced here: 39.8 us
  blocking collectives  30.5 us (76%)
  Pallas kernels  7.37 us (18%)
  waiting for transfers between devices  1.22 us (3%)
  between operations  0.66 us (2%)
    all_to_all x1, blocking collectives, per_device(): got = lax.all_to_all(blocks, ('chip', 'core', 'mp'), 0, 0, tiled=True)  17.8 us
    all_to_all x1, blocking collectives, per_device(): parts = lax.all_to_all(parts, ('chip', 'mp'), 0, 0, tiled=True)  12.7 us
    pallas_call x1, Pallas kernels, pool_call(): pl.pallas_call(functools.partial(pool_kernel, owners=owners, peers=peers,...  4.11 us
    pallas_call x1, Pallas kernels, per_device(): pl.pallas_call(functools.partial(project_kernel, owners=owners, peers=pee...  2.29 us
    ppermute x1, waiting for transfers between devices, per_device(): lax.ppermute(other, 'core', [(c, (c + 1) % CORES) for c in range(CORES)])  1.22 us
  transfers between devices with their start and end apart: 1, of which 1 were waited for; matrix products, arithmetic and copies ran while one was open for 0% of the time, Pallas kernels for 0%

profile of v8, /device:TPU:0, one launch (start us, length us, event | category | flops | bytes accessed | tf_op | source)
XLA Modules:
  0.0 39.8 jit_solution(2344605948056604789)
XLA Ops:
  0.6 4.1 %pool.1 = (bf16[32,2,1664]{2,1,0:T(2,128)(2,1)S(1)}, bf16[512,256]{1,0:T(8,128)(2,1)S(1)}) custom-call(s32[6]{0:T(128)} %lens_hbm.1, s32[24]{0:T(128)} %ids_hbm.1, bf16[6,256,4096]{2,1,0:T(8,128)(2,1)} %hidden.1, s32[512,128]{1,0:T(8,128)} %bitcast.3, bf16[32,128]{1,0:T(8,128)(2,1)} %bitcast.4, bf16[512,256]{1,0:T(8,128)(2,1)} %head.1), custom_call_target="tpu_custom_call" | custom-call | tf_op jit(solution)/shard_map/pool/pallas_call | solution.py:362
  4.8 17.8 %all_to_all.10.got = bf16[32,2,1664]{2,1,0:T(2,128)(2,1)S(1)} all-to-all(bf16[32,2,1664]{2,1,0:T(2,128)(2,1)S(1)} %get-tuple-element.9), channel_id=1, replica_groups=mesh['chip'=4,'core'=2,'mp'=4] {'chip','core','mp'}, dimensions={0} | all-to-all | bytes 425984 | tf_op jit(solution)/shard_map/all_to_all | solution.py:408
  22.5 2.3 %project.1 = (f32[96,256]{1,0:T(8,128)S(1)}, bf16[96,256]{1,0:T(8,128)(2,1)S(1)}, bf16[256,1024]{1,0:T(8,128)(2,1)S(1)}) custom-call(bf16[32,2,1664]{2,1,0:T(2,128)(2,1)S(1)} %all_to_all.10.got, bf16[512,256]{1,0:T(8,128)(2,1)S(1)} %get-tuple-element.10.head, bf16[8192,1024]{1,0:T(8,128)(2,1)} %cents.1, bf16[256,1024]{1,0:T(8,128)(2,1)} %rotation.1), custom_call_target="tpu_custom_call" | custom-call | tf_op jit(solution)/shard_map/project/pallas_call | solution.py:410
  24.8 0.1 collective-permute-start
  24.9 1.2 %collective-permute-done.other = bf16[96,256]{1,0:T(8,128)(2,1)S(1)} collective-permute-done((bf16[96,256]{1,0:T(8,128)(2,1)S(1)}, bf16[96,256]{1,0:T(8,128)(2,1)S(1)}, u32[]{:S(2)}, u32[]{:S(2)}) %collective-permute-start) | collective-permute-done | bytes 49184 | tf_op jit(solution)/shard_map/ppermute | solution.py:432
  26.1 0.2 rotate.1
  26.3 12.7 %all_to_all.11.parts = bf16[16,24,256]{2,1,0:T(8,128)(2,1)S(1)} all-to-all(bf16[16,24,256]{2,1,0:T(8,128)(2,1)S(1)} %rotate.1), channel_id=1, replica_groups=mesh['chip'=4,'core'=2,'mp'=4] {'chip','mp'}, dimensions={0} | all-to-all | bytes 393216 | tf_op jit(solution)/shard_map/all_to_all | solution.py:441
  39.0 0.8 %quantize.1 = (bf16[24,256]{1,0:T(8,128)(2,1)}, bf16[4,24]{1,0:T(4,128)(2,1)}) custom-call(bf16[16,24,256]{2,1,0:T(8,128)(2,1)S(1)} %all_to_all.11.parts), custom_call_target="tpu_custom_call" | custom-call | tf_op jit(solution)/shard_map/quantize/pallas_call | solution.py:442
Async XLA Ops:
  24.8 1.3 %collective-permute-start = (bf16[96,256]{1,0:T(8,128)(2,1)S(1)}, bf16[96,256]{1,0:T(8,128)(2,1)S(1)}, u32[]{:S(2)}, u32[]{:S(2)}) collective-permute-start(bf16[96,256]{1,0:T(8,128)(2,1)S(1)} %get-tuple-element.12), channel_id=1, source_target_pairs={{0,4},{4,0},{1,5},{5,1},{2,6},{6,2},{3,7},{7,3},{8,12},{12,8},{9,1... | collective-permute-start | bytes 147464 | tf_op jit(solution)/shard_map/ppermute | solution.py:432

commit v9 on v8

--- a/solution.py
+++ b/solution.py
@@ -59,6 +59,9 @@
     for p in range(passes):
         chunk_copy(p, 0).start()
         items[p] = p * steps
+    side[1].wait()
+    for g in range(group):
+        slot_copy(g).start()
     side[0].wait()
     count = jnp.int32(passes)
     for c in range(1, steps):
@@ -71,9 +74,6 @@
                 items[count] = p * steps + c
 
             count = count + needed.astype(jnp.int32)
-    side[1].wait()
-    for g in range(group):
-        slot_copy(g).start()
     side[2].start()
     side[3].start()
 

time: 40 us -> 39.2 us (0.980)
  blocking collectives: 30.5 us -> 28.7 us
  Pallas kernels: 7.37 us -> 8.28 us
    all_to_all x1, blocking collectives: 17.8 us -> 15.9 us  [per_device(): got = lax.all_to_all(blocks, ('chip', 'core', 'mp'), 0, 0, tiled=True)]
    pallas_call x1, Pallas kernels: 4.11 us -> 5.08 us  [pool_call(): pl.pallas_call(functools.partial(pool_kernel, owners=owners, peers=peers,...]
where the time goes in v9:
time: 39.2 us; the launch traced here: 38.9 us
  blocking collectives  28.7 us (73%)
  Pallas kernels  8.28 us (21%)
  waiting for transfers between devices  1.22 us (3%)
  between operations  0.66 us (2%)
    all_to_all x1, blocking collectives, per_device(): got = lax.all_to_all(blocks, ('chip', 'core', 'mp'), 0, 0, tiled=True)  15.9 us
    all_to_all x1, blocking collectives, per_device(): parts = lax.all_to_all(parts, ('chip', 'mp'), 0, 0, tiled=True)  12.8 us
    pallas_call x1, Pallas kernels, pool_call(): pl.pallas_call(functools.partial(pool_kernel, owners=owners, peers=peers,...  5.08 us
    pallas_call x1, Pallas kernels, per_device(): pl.pallas_call(functools.partial(project_kernel, owners=owners, peers=pee...  2.23 us
    ppermute x1, waiting for transfers between devices, per_device(): lax.ppermute(other, 'core', [(c, (c + 1) % CORES) for c in range(CORES)])  1.22 us
  transfers between devices with their start and end apart: 1, of which 1 were waited for; matrix products, arithmetic and copies ran while one was open for 0% of the time, Pallas kernels for 0%

profile of v9, /device:TPU:0, one launch (start us, length us, event | category | flops | bytes accessed | tf_op | source)
XLA Modules:
  0.0 38.9 jit_solution(11657153067844846329)
XLA Ops:
  0.6 5.1 %pool.1 = (bf16[32,2,1664]{2,1,0:T(2,128)(2,1)S(1)}, bf16[512,256]{1,0:T(8,128)(2,1)S(1)}) custom-call(s32[6]{0:T(128)} %lens_hbm.1, s32[24]{0:T(128)} %ids_hbm.1, bf16[6,256,4096]{2,1,0:T(8,128)(2,1)} %hidden.1, s32[512,128]{1,0:T(8,128)} %bitcast.3, bf16[32,128]{1,0:T(8,128)(2,1)} %bitcast.4, bf16[512,256]{1,0:T(8,128)(2,1)} %head.1), custom_call_target="tpu_custom_call" | custom-call | tf_op jit(solution)/shard_map/pool/pallas_call | solution.py:362
  5.7 15.9 %all_to_all.10.got = bf16[32,2,1664]{2,1,0:T(2,128)(2,1)S(1)} all-to-all(bf16[32,2,1664]{2,1,0:T(2,128)(2,1)S(1)} %get-tuple-element.9), channel_id=1, replica_groups=mesh['chip'=4,'core'=2,'mp'=4] {'chip','core','mp'}, dimensions={0} | all-to-all | bytes 425984 | tf_op jit(solution)/shard_map/all_to_all | solution.py:408
  21.6 2.2 %project.1 = (f32[96,256]{1,0:T(8,128)S(1)}, bf16[96,256]{1,0:T(8,128)(2,1)S(1)}, bf16[256,1024]{1,0:T(8,128)(2,1)S(1)}) custom-call(bf16[32,2,1664]{2,1,0:T(2,128)(2,1)S(1)} %all_to_all.10.got, bf16[512,256]{1,0:T(8,128)(2,1)S(1)} %get-tuple-element.10.head, bf16[8192,1024]{1,0:T(8,128)(2,1)} %cents.1, bf16[256,1024]{1,0:T(8,128)(2,1)} %rotation.1), custom_call_target="tpu_custom_call" | custom-call | tf_op jit(solution)/shard_map/project/pallas_call | solution.py:410
  23.9 0.1 collective-permute-start
  23.9 1.2 %collective-permute-done.other = bf16[96,256]{1,0:T(8,128)(2,1)S(1)} collective-permute-done((bf16[96,256]{1,0:T(8,128)(2,1)S(1)}, bf16[96,256]{1,0:T(8,128)(2,1)S(1)}, u32[]{:S(2)}, u32[]{:S(2)}) %collective-permute-start) | collective-permute-done | bytes 49184 | tf_op jit(solution)/shard_map/ppermute | solution.py:432
  25.1 0.2 rotate.1
  25.4 12.8 %all_to_all.11.parts = bf16[16,24,256]{2,1,0:T(8,128)(2,1)S(1)} all-to-all(bf16[16,24,256]{2,1,0:T(8,128)(2,1)S(1)} %rotate.1), channel_id=1, replica_groups=mesh['chip'=4,'core'=2,'mp'=4] {'chip','mp'}, dimensions={0} | all-to-all | bytes 393216 | tf_op jit(solution)/shard_map/all_to_all | solution.py:441
  38.2 0.8 %quantize.1 = (bf16[24,256]{1,0:T(8,128)(2,1)}, bf16[4,24]{1,0:T(4,128)(2,1)}) custom-call(bf16[16,24,256]{2,1,0:T(8,128)(2,1)S(1)} %all_to_all.11.parts), custom_call_target="tpu_custom_call" | custom-call | tf_op jit(solution)/shard_map/quantize/pallas_call | solution.py:442
Async XLA Ops:
  23.9 1.3 %collective-permute-start = (bf16[96,256]{1,0:T(8,128)(2,1)S(1)}, bf16[96,256]{1,0:T(8,128)(2,1)S(1)}, u32[]{:S(2)}, u32[]{:S(2)}) collective-permute-start(bf16[96,256]{1,0:T(8,128)(2,1)S(1)} %get-tuple-element.12), channel_id=1, source_target_pairs={{0,4},{4,0},{1,5},{5,1},{2,6},{6,2},{3,7},{7,3},{8,12},{12,8},{9,1... | collective-permute-start | bytes 147464 | tf_op jit(solution)/shard_map/ppermute | solution.py:432

commit v10 on v8

--- a/solution.py
+++ b/solution.py
@@ -125,8 +125,8 @@
     weigh(jnp.int32(0))
 
     def body(k, _):
+        add(k)
         arrive(k + 1)
-        add(k)
         weigh(k + 1)
         return 0
 

time: 40 us -> 39.7 us (level)
  blocking collectives: 30.5 us -> 28.3 us
  Pallas kernels: 7.37 us -> 9.52 us
    pallas_call x1, Pallas kernels: 4.11 us -> 6.33 us  [pool_call(): pl.pallas_call(functools.partial(pool_kernel, owners=owners, peers=peers,...]
    all_to_all x1, blocking collectives: 17.8 us -> 15.8 us  [per_device(): got = lax.all_to_all(blocks, ('chip', 'core', 'mp'), 0, 0, tiled=True)]
where the time goes in v10:
time: 39.7 us; the launch traced here: 39.8 us
  blocking collectives  28.3 us (71%)
  Pallas kernels  9.52 us (24%)
  waiting for transfers between devices  1.22 us (3%)
  between operations  0.66 us (2%)
    all_to_all x1, blocking collectives, per_device(): got = lax.all_to_all(blocks, ('chip', 'core', 'mp'), 0, 0, tiled=True)  15.8 us
    all_to_all x1, blocking collectives, per_device(): parts = lax.all_to_all(parts, ('chip', 'mp'), 0, 0, tiled=True)  12.6 us
    pallas_call x1, Pallas kernels, pool_call(): pl.pallas_call(functools.partial(pool_kernel, owners=owners, peers=peers,...  6.33 us
    pallas_call x1, Pallas kernels, per_device(): pl.pallas_call(functools.partial(project_kernel, owners=owners, peers=pee...  2.22 us
    ppermute x1, waiting for transfers between devices, per_device(): lax.ppermute(other, 'core', [(c, (c + 1) % CORES) for c in range(CORES)])  1.22 us
  transfers between devices with their start and end apart: 1, of which 1 were waited for; matrix products, arithmetic and copies ran while one was open for 0% of the time, Pallas kernels for 0%

profile of v10, /device:TPU:0, one launch (start us, length us, event | category | flops | bytes accessed | tf_op | source)
XLA Modules:
  0.0 39.8 jit_solution(6728096079769140786)
XLA Ops:
  0.6 6.3 %pool.1 = (bf16[32,2,1664]{2,1,0:T(2,128)(2,1)S(1)}, bf16[512,256]{1,0:T(8,128)(2,1)S(1)}) custom-call(s32[6]{0:T(128)} %lens_hbm.1, s32[24]{0:T(128)} %ids_hbm.1, bf16[6,256,4096]{2,1,0:T(8,128)(2,1)} %hidden.1, s32[512,128]{1,0:T(8,128)} %bitcast.3, bf16[32,128]{1,0:T(8,128)(2,1)} %bitcast.4, bf16[512,256]{1,0:T(8,128)(2,1)} %head.1), custom_call_target="tpu_custom_call" | custom-call | tf_op jit(solution)/shard_map/pool/pallas_call | solution.py:362
  7.0 15.8 %all_to_all.10.got = bf16[32,2,1664]{2,1,0:T(2,128)(2,1)S(1)} all-to-all(bf16[32,2,1664]{2,1,0:T(2,128)(2,1)S(1)} %get-tuple-element.9), channel_id=1, replica_groups=mesh['chip'=4,'core'=2,'mp'=4] {'chip','core','mp'}, dimensions={0} | all-to-all | bytes 425984 | tf_op jit(solution)/shard_map/all_to_all | solution.py:408
  22.7 2.2 %project.1 = (f32[96,256]{1,0:T(8,128)S(1)}, bf16[96,256]{1,0:T(8,128)(2,1)S(1)}, bf16[256,1024]{1,0:T(8,128)(2,1)S(1)}) custom-call(bf16[32,2,1664]{2,1,0:T(2,128)(2,1)S(1)} %all_to_all.10.got, bf16[512,256]{1,0:T(8,128)(2,1)S(1)} %get-tuple-element.10.head, bf16[8192,1024]{1,0:T(8,128)(2,1)} %cents.1, bf16[256,1024]{1,0:T(8,128)(2,1)} %rotation.1), custom_call_target="tpu_custom_call" | custom-call | tf_op jit(solution)/shard_map/project/pallas_call | solution.py:410
  25.0 0.1 collective-permute-start
  25.1 1.2 %collective-permute-done.other = bf16[96,256]{1,0:T(8,128)(2,1)S(1)} collective-permute-done((bf16[96,256]{1,0:T(8,128)(2,1)S(1)}, bf16[96,256]{1,0:T(8,128)(2,1)S(1)}, u32[]{:S(2)}, u32[]{:S(2)}) %collective-permute-start) | collective-permute-done | bytes 49184 | tf_op jit(solution)/shard_map/ppermute | solution.py:432
  26.3 0.2 rotate.1
  26.5 12.6 %all_to_all.11.parts = bf16[16,24,256]{2,1,0:T(8,128)(2,1)S(1)} all-to-all(bf16[16,24,256]{2,1,0:T(8,128)(2,1)S(1)} %rotate.1), channel_id=1, replica_groups=mesh['chip'=4,'core'=2,'mp'=4] {'chip','mp'}, dimensions={0} | all-to-all | bytes 393216 | tf_op jit(solution)/shard_map/all_to_all | solution.py:441
  39.0 0.8 %quantize.1 = (bf16[24,256]{1,0:T(8,128)(2,1)}, bf16[4,24]{1,0:T(4,128)(2,1)}) custom-call(bf16[16,24,256]{2,1,0:T(8,128)(2,1)S(1)} %all_to_all.11.parts), custom_call_target="tpu_custom_call" | custom-call | tf_op jit(solution)/shard_map/quantize/pallas_call | solution.py:442
Async XLA Ops:
  25.0 1.3 %collective-permute-start = (bf16[96,256]{1,0:T(8,128)(2,1)S(1)}, bf16[96,256]{1,0:T(8,128)(2,1)S(1)}, u32[]{:S(2)}, u32[]{:S(2)}) collective-permute-start(bf16[96,256]{1,0:T(8,128)(2,1)S(1)} %get-tuple-element.12), channel_id=1, source_target_pairs={{0,4},{4,0},{1,5},{5,1},{2,6},{6,2},{3,7},{7,3},{8,12},{12,8},{9,1... | collective-permute-start | bytes 147464 | tf_op jit(solution)/shard_map/ppermute | solution.py:432
